TPU v7x, 32 devices: a whole 2x2x4 slice. The times are simulated.
32 devices in a mesh: dp: 16 (over z, x, core), tensor: 2 (over y).
Axes of the slice: x: 2, y: 2, z: 4, core: 2. Of those that a mesh axis runs over, the one named last changes fastest.
Arguments:
- tokens: bfloat16 [32768, 768], P(('dp', 'tensor')), may hold values from -6 to 6
- segment_ids: int32 [16, 2048], P('dp'), may hold values from 0 to 15, never falling along the last dimension, each value on 1 to 1024 neighbouring positions
- ln1_gain: bfloat16 [768], P('dp'), may hold values from 0.25 to 1.75
- ln1_bias: bfloat16 [768], P('dp'), may hold values from -1.796875 to 1.796875
- w_qkv: bfloat16 [768, 3, 768], P('dp', None, 'tensor'), may hold values from -0.3125 to 0.3125
- b_qv: bfloat16 [2, 768], P(None, 'dp'), may hold values from -1.796875 to 1.796875
- w_attn_out: bfloat16 [768, 768], P('tensor', 'dp'), may hold values from -3 to 3
- b_attn_out: bfloat16 [768], P('dp'), may hold values from -6 to 6
- ln2_gain: bfloat16 [768], P('dp'), may hold values from 0.25 to 1.75
- ln2_bias: bfloat16 [768], P('dp'), may hold values from -1.796875 to 1.796875
- w_fc: bfloat16 [768, 3072], P('dp', 'tensor'), may hold values from -0.21875 to 0.21875
- b_fc: bfloat16 [3072], P('dp'), may hold values from -1.796875 to 1.796875
- w_proj: bfloat16 [3072, 768], P('tensor', 'dp'), may hold values from -0.8984375 to 0.8984375
- b_proj: bfloat16 [768], P('dp'), may hold values from -6 to 6
- cotangent: bfloat16 [32768, 768], P(('dp', 'tensor')), may hold values from -6 to 6
Outputs:
- block_out: bfloat16 [32768, 768], P(('dp', 'tensor'))
- grad_tokens: bfloat16 [32768, 768], P(('dp', 'tensor'))
- grad_ln1_gain: float32 [768], P('dp')
- grad_ln1_bias: float32 [768], P('dp')
- grad_w_qkv: float32 [768, 3, 768], P('dp', None, 'tensor')
- grad_b_qv: float32 [2, 768], P(None, 'dp')
- grad_w_attn_out: float32 [768, 768], P('tensor', 'dp')
- grad_b_attn_out: float32 [768], P('dp')
- grad_ln2_gain: float32 [768], P('dp')
- grad_ln2_bias: float32 [768], P('dp')
- grad_w_fc: float32 [768, 3072], P('dp', 'tensor')
- grad_b_fc: float32 [3072], P('dp')
- grad_w_proj: float32 [3072, 768], P('tensor', 'dp')
- grad_b_proj: float32 [768], P('dp')
Inputs may be any that keep to these rules, and one draw needn't show every extreme that they name: `segment_ids`: in each sequence the document numbers never fall; each document has 1 to 1024 tokens, and one has exactly 1024.
All inputs are finite; a program needn't handle non-finite values.
Results may differ from a plain program's by a relative error of at most 0.02.
Values may be sent and summed in bfloat16 or wider, within the bound.
A program may use at most 256 MiB of HBM per device.

v0:
```python
import functools

import jax
import jax.numpy as jnp
from jax import lax
from jax.experimental import pallas as pl
from jax.experimental.pallas import tpu as pltpu
from jax.sharding import PartitionSpec as P

HD = 64
QB = 256
NEG = -1e30
EPSILON = 1e-05
BRANCH_SCALE = 48.0 ** (-0.5)
SMALL = 128
VECS = 16
ROWS = 256
HIDDEN = 512
bf = jnp.bfloat16
f32 = jnp.float32
NT = (((1,), (1,)), ((), ()))
TN = (((0,), (0,)), ((), ()))
BOTH = ("dp", "tensor")
MESH_ID = pl.DeviceIdType.MESH
ANY = pl.BlockSpec(memory_space=pl.ANY)
VM = pl.BlockSpec(memory_space=pltpu.VMEM)
SM = pl.BlockSpec(memory_space=pltpu.SMEM)


def attn_info(seg, core):
    n=seg.shape[0]; nb=n//QB
    docs=jnp.arange(16,dtype=jnp.int32)
    first=jnp.sum((seg[None,:]<docs[:,None]).astype(jnp.int32),axis=1)
    starts=jnp.sum(jnp.where(seg[None,:]==docs[:,None],first[:,None],0),axis=0)
    blocks=starts.reshape(nb,QB)
    idx=jnp.arange(nb,dtype=jnp.int32)
    low=blocks[:,0]//QB
    mid=jnp.clip((blocks[:,QB-1]+QB-1)//QB,low,idx)
    return starts.reshape(1,n), jnp.concatenate([jnp.reshape(core,(1,)),low,mid]).astype(jnp.int32)

def attn_masks(kat, srow, diagonal):
    keys = lax.broadcasted_iota(jnp.int32, (QB, QB), 0)
    mask = keys >= (srow - kat)
    if diagonal:
        mask = mask & (keys <= lax.broadcasted_iota(jnp.int32, (QB, QB), 1))
    return mask


def head_lanes(values):
    low = (lax.broadcasted_iota(jnp.int32, (1, values.shape[1]), 1) % 128) < HD
    zero = jnp.zeros((), bf)
    return jnp.where(low, values, zero), jnp.where(low, zero, values)


def fwd_kernel(info, own, recv, st_ref, okeep, osend, lse_ref, qm, ks, vt, osc, acc):
    half, cols = own.shape[0], own.shape[1] // 3
    n, nb, heads, pairs = 2 * half, 2 * half // QB, cols // HD, cols // 128
    c = info[0]
    for base, src in ((c * half, own), ((1 - c) * half, recv)):
        rows = pl.ds(pl.multiple_of(base, half), half)
        for g in range(pairs):
            lanes = slice(g * 128, (g + 1) * 128)
            part = lambda k: src[:, (3 * g + k) * 128 : (3 * g + k + 1) * 128]
            qm[0, rows, lanes], qm[1, rows, lanes] = head_lanes(part(0) * bf(HD**-0.5))
            ks[rows, lanes] = part(1)
            vt[lanes, rows] = part(2).T

    def qblock(i, _):
        at = pl.multiple_of(i * QB, QB)
        qr = pl.ds(at, QB)
        srow = st_ref[:, qr]
        acc[...] = jnp.zeros_like(acc)

        def step(mode, j, carry):
            kat = pl.multiple_of(j * QB, QB)
            kr = pl.ds(kat, QB)
            if mode:
                mask = attn_masks(kat, srow, mode == 2)
            scores, mixed = [], []
            for h in range(heads):
                lanes = slice(h // 2 * 128, h // 2 * 128 + 128)
                one = lax.dot_general(ks[kr, lanes], qm[h % 2, qr, lanes], NT, preferred_element_type=f32)
                scores.append(jnp.where(mask, one, NEG) if mode else one)
            for h in range(heads):
                top, total = carry[h]
                new = jnp.maximum(top, jnp.max(scores[h], axis=0, keepdims=True))
                weights = jnp.exp(scores[h] - new)
                fade = jnp.exp(top - new)
                total = fade * total + jnp.sum(weights, axis=0, keepdims=True)
                mixed.append((new, total, fade, weights.astype(bf)))
            for h in range(heads):
                sub = slice(h * HD, (h + 1) * HD)
                acc[sub] = mixed[h][2] * acc[sub] + jnp.dot(vt[sub, kr], mixed[h][3], preferred_element_type=f32)
            return tuple(m[:2] for m in mixed)

        carry = step(2, i, ((jnp.full((1, QB), NEG, f32), jnp.zeros((1, QB), f32)),) * heads)
        carry = lax.fori_loop(info[1 + i], info[1 + nb + i], functools.partial(step, 1), carry)
        carry = lax.fori_loop(info[1 + nb + i], i, functools.partial(step, 0), carry)
        for h, (top, total) in enumerate(carry):
            sub = slice(h * HD, (h + 1) * HD)
            acc[sub] = acc[sub] / total
            lse_ref[h : h + 1, qr] = top + jnp.log(total)
        osc[qr] = acc[...].T.astype(bf)
        return 0

    lax.fori_loop(0, nb, qblock, 0)
    okeep[...] = osc[pl.ds(pl.multiple_of(c * half, half), half)]
    osend[...] = osc[pl.ds(pl.multiple_of((1 - c) * half, half), half)]


def attn_fwd(own, recv, starts, info):
    half, cols = own.shape[0], own.shape[1] // 3
    n = 2 * half
    return pl.pallas_call(
        fwd_kernel,
        in_specs=[SM, VM, VM, VM],
        out_specs=[VM] * 3,
        scratch_shapes=[
            pltpu.VMEM((2, n, cols), bf), pltpu.VMEM((n, cols), bf), pltpu.VMEM((cols, n), bf),
            pltpu.VMEM((n, cols), bf), pltpu.VMEM((cols, QB), f32)],
        out_shape=[jax.ShapeDtypeStruct((half, cols), bf)] * 2 + [jax.ShapeDtypeStruct((cols // HD, n), f32)],
        cost_estimate=pl.CostEstimate(flops=n * n, bytes_accessed=n * 128, transcendentals=0),
        compiler_params=pltpu.CompilerParams(vmem_limit_bytes=48 << 20),
    )(info, own, recv, starts)


def bwd_kernel(info, own, recv, doo, dor, oo, orr, st_ref, lse_ref, dkeep, dsend, qm, ks, vs, kt, dom, dlt, dqs, dks, dvs):
    half, cols = own.shape[0], own.shape[1] // 3
    n, nb, heads, pairs = 2 * half, 2 * half // QB, cols // HD, cols // 128
    c = info[0]
    lanes_of = lambda g: slice(g * 128, (g + 1) * 128)
    for base, src, do, o in ((c * half, own, doo, oo), ((1 - c) * half, recv, dor, orr)):
        rows = pl.ds(pl.multiple_of(base, half), half)
        for g in range(pairs):
            lanes = lanes_of(g)
            part = lambda k: src[:, (3 * g + k) * 128 : (3 * g + k + 1) * 128]
            qm[0, rows, lanes], qm[1, rows, lanes] = head_lanes(part(0) * bf(HD**-0.5))
            ks[rows, lanes] = part(1)
            vs[rows, lanes] = part(2)
            kt[lanes, rows] = part(1).T
            grad = do[:, lanes]
            dom[0, rows, lanes], dom[1, rows, lanes] = head_lanes(grad)
            prod = (grad.astype(f32) * o[:, lanes].astype(f32)).T
            for e in range(2):
                dlt[2 * g + e : 2 * g + e + 1, rows] = jnp.sum(prod[e * HD : (e + 1) * HD], axis=0, keepdims=True)
    dks[...] = jnp.zeros_like(dks)
    dvs[...] = jnp.zeros_like(dvs)

    def qblock(i, _):
        at = pl.multiple_of(i * QB, QB)
        qr = pl.ds(at, QB)
        srow = st_ref[:, qr]
        dqs[...] = jnp.zeros_like(dqs)

        def step(mode, j, carry):
            kat = pl.multiple_of(j * QB, QB)
            kr = pl.ds(kat, QB)
            if mode:
                mask = attn_masks(kat, srow, mode == 2)
            scores, softs, grads = [], [], []
            for h in range(heads):
                lanes = lanes_of(h // 2)
                one = lax.dot_general(ks[kr, lanes], qm[h % 2, qr, lanes], NT, preferred_element_type=f32)
                back = lax.dot_general(vs[kr, lanes], dom[h % 2, qr, lanes], NT, preferred_element_type=f32)
                scores.append((jnp.where(mask, one, NEG) if mode else one, back))
            for h in range(heads):
                soft = jnp.exp(scores[h][0] - lse_ref[h : h + 1, qr])
                grads.append((soft * (scores[h][1] - dlt[h : h + 1, qr])).astype(bf))
                softs.append(soft.astype(bf))
            for g in range(pairs):
                lanes = lanes_of(g)
                both = lambda ref: jnp.concatenate([ref[0, qr, lanes], ref[1, qr, lanes]], axis=0)
                two = slice(2 * g, 2 * g + 2)
                dvs[kr, lanes] += jnp.dot(jnp.concatenate(softs[two], axis=1), both(dom), preferred_element_type=f32)
                dks[kr, lanes] += jnp.dot(jnp.concatenate(grads[two], axis=1), both(qm), preferred_element_type=f32)
                for h in (2 * g, 2 * g + 1):
                    sub = slice(h * HD, (h + 1) * HD)
                    dqs[sub] += jnp.dot(kt[sub, kr], grads[h], preferred_element_type=f32)
            return carry

        step(2, i, 0)
        lax.fori_loop(info[1 + i], info[1 + nb + i], functools.partial(step, 1), 0)
        lax.fori_loop(info[1 + nb + i], i, functools.partial(step, 0), 0)
        qm[0, qr] = (dqs[...] * (HD**-0.5)).T.astype(bf)
        return 0

    lax.fori_loop(0, nb, qblock, 0)
    for dst, base in ((dkeep, c * half), (dsend, (1 - c) * half)):
        rows = pl.ds(pl.multiple_of(base, half), half)
        for g in range(pairs):
            for k, value in enumerate((qm[0, rows, lanes_of(g)], dks[rows, lanes_of(g)], dvs[rows, lanes_of(g)])):
                dst[:, (3 * g + k) * 128 : (3 * g + k + 1) * 128] = value.astype(bf)


def attn_bwd(own, recv, do_own, do_recv, o_own, o_recv, starts, lse, info):
    half, cols = own.shape[0], own.shape[1] // 3
    n = 2 * half
    return pl.pallas_call(
        bwd_kernel,
        in_specs=[SM] + [VM] * 8,
        out_specs=[VM] * 2,
        scratch_shapes=[
            pltpu.VMEM((2, n, cols), bf), pltpu.VMEM((n, cols), bf), pltpu.VMEM((n, cols), bf), pltpu.VMEM((cols, n), bf),
            pltpu.VMEM((2, n, cols), bf), pltpu.VMEM((cols // HD, n), f32), pltpu.VMEM((cols, QB), f32),
            pltpu.VMEM((n, cols), f32), pltpu.VMEM((n, cols), f32)],
        out_shape=[like((half, 3 * cols), bf)] * 2,
        cost_estimate=pl.CostEstimate(flops=n * n, bytes_accessed=n * 128, transcendentals=0),
        compiler_params=pltpu.CompilerParams(vmem_limit_bytes=56 << 20),
    )(info, own, recv, do_own, do_recv, o_own, o_recv, starts, lse)


def dot(left, right, dims=(((1,), (0,)), ((), ()))):
    return lax.dot_general(left, right, dims, preferred_element_type=f32)


def exchange(value, bit, dp_size):
    if bit:
        return lax.ppermute(value, "dp", [(i, i ^ bit) for i in range(dp_size)])
    return lax.ppermute(value, "tensor", [(0, 1), (1, 0)])


def flip(index, bits):
    for bit in bits:
        index = index + bit * (1 - 2 * ((index // bit) % 2))
    return index

def far_groups(dp_size):
    far = [1 << k for k in range(dp_size.bit_length() - 2, 1, -1)]
    return [tuple(far[k : k + 2]) for k in range(0, len(far), 2)]

def group_moves(group):
    if len(group) == 1:
        return [(1, group)]
    return [(1, group[:1]), (2, group[1:]), (3, group)]

def chunks_of(cols, which, count, until=None):
    tiles = cols // 128
    cuts = [128 * ((tiles * k) // count) for k in range(count + 1)]
    arrays = range(which, until + 1) if until else (which,)
    return tuple(
        (array, low, high - low, 128 * max(1, (high - low) * 2 // 3 // 128))
        for low, high in zip(cuts, cuts[1:]) for array in arrays)


def head_kernel(groups, chunks, tokens, *refs):
    shards, x_out, outs, (send_sem, recv_sem, local_sem) = refs[:4], refs[4], refs[5:9], refs[9:]
    dp, t = lax.axis_index("dp"), lax.axis_index("tensor")
    core = dp % 2
    away = core + t - 2 * core * t
    near = {1: (flip(dp, (1,)), t), 2: (flip(dp, (2,)), t), 0: (dp, 1 - t)}
    distant = [bits for group in groups for _, bits in group_moves(group)]
    swap = (dp - core + t, core)
    barrier = pltpu.get_barrier_semaphore()
    for device in list(near.values()) + [(flip(dp, bits), t) for bits in distant]:
        pl.semaphore_signal(barrier, inc=1, device_id=device, device_id_type=MESH_ID)

    @pl.when(away == 1)
    def _():
        pl.semaphore_signal(barrier, inc=1, device_id=swap, device_id_type=MESH_ID)

    local = [
        pltpu.make_async_copy(shards[k], outs[k].at[away, 0] if k < 2 else outs[k].at[0], local_sem.at[k]) for k in range(4)]
    for copy in local:
        copy.start()
    pl.semaphore_wait(barrier, len(near) + len(distant) + away)
    count = [0]

    def remote(src, dst, device):
        slot = count[0]
        count[0] += 1
        return pltpu.make_async_remote_copy(
            src_ref=src, dst_ref=dst, send_sem=send_sem.at[slot], recv_sem=recv_sem.at[slot],
            device_id=device, device_id_type=MESH_ID)

    def blocks(ref, index, first, held, low, size):
        return ref.at[index, pl.ds(first, held), :, pl.ds(low, size)]

    plans = []
    for which, low, size, part in chunks:
        shard, out = shards[which], outs[which]
        steps, held = [], 1
        for group in groups:
            moves = []
            for place, bits in group_moves(group):
                src = shard.at[:, pl.ds(low, size)] if held == 1 else blocks(out, away, 0, held, low, size)
                dst = out.at[away, place, :, pl.ds(low, size)] if held == 1 else blocks(out, away, place * held, held, low, size)
                moves.append(remote(src, dst, (flip(dp, bits), t)))
            held *= len(group_moves(group)) + 1
            steps.append(moves)
        a, b = (low, part), (low + part, size - part)
        steps.append([
            remote(blocks(out, away, 0, held, *a), blocks(out, away, 0, held, *a), near[0]),
            remote(blocks(out, away, 0, held, *b), blocks(out, away, held, held, *b), near[2]),
        ])
        steps.append(
            [remote(blocks(out, k, 0, held, *a), blocks(out, k, held, held, *a), near[2]) for k in range(2)]
            + [remote(blocks(out, away, 0, 2 * held, *b), blocks(out, away, 0, 2 * held, *b), near[0])])
        steps.append([
            remote(blocks(out, k, 0, 2 * held, low, size),
                   blocks(out, 1 - k, 2 * held, 2 * held, low, size), near[1]) for k in range(2)])
        plans.append(steps)
    later = []
    held = 1
    for group in groups:
        moves = []
        for place, bits in group_moves(group):
            for shard, out in zip(shards[2:], outs[2:]):
                src = shard if held == 1 else out.at[pl.ds(0, held)]
                dst = out.at[place] if held == 1 else out.at[pl.ds(place * held, held)]
                moves.append(remote(src, dst, (flip(dp, bits), t)))
        held *= len(group_moves(group)) + 1
        later.append(moves)
    depth = len(plans[0])
    swap_copy = remote(tokens, x_out, swap)
    stay_copy = pltpu.make_async_copy(tokens, x_out, local_sem.at[4])
    waited = set()

    def advance(number, phase):
        if number >= len(plans):
            return
        if phase > 0:
            for move in plans[number][phase - 1]:
                move.wait_recv()
        if phase == 1 and chunks[number][0] not in waited:
            waited.add(chunks[number][0])
            local[chunks[number][0]].wait()
        if phase < depth:
            for move in plans[number][phase]:
                move.start()

    advance(0, 0)

    @pl.when(away == 1)
    def _():
        swap_copy.start()

    @pl.when(away == 0)
    def _():
        stay_copy.start()

    far = len(groups)
    for number in range(len(plans)):
        if number == 0:
            for phase in range(1, far + 1):
                advance(0, phase)
            advance(1, 0)
        advance(number, far + 1)
        for phase in range(1, far + 1):
            advance(number + 1, phase)
        advance(number + 2, 0)
        if number == len(plans) - 2:
            for move in later[0]:
                move.start()
        advance(number, far + 2)
    for number in range(len(plans)):
        advance(number, depth)

    @pl.when(away == 1)
    def _():
        swap_copy.wait()

    @pl.when(away == 0)
    def _():
        stay_copy.wait()

    for which in sorted(set(range(4)) - waited):
        local[which].wait()
    for k, moves in enumerate(later):
        if k > 0:
            for move in moves:
                move.start()
        for move in moves:
            move.wait()
    for steps in plans:
        for moves in steps:
            for move in moves:
                move.wait_send()


def head(dp_size, tokens, shards, chunks):
    groups = far_groups(dp_size)
    partners = sum(len(group_moves(g)) for g in groups)
    slots = len(chunks) * (partners + 7) + 2 * partners + 1
    shapes = [(2, dp_size)] * 2 + [(dp_size // 4,)] * 2
    return pl.pallas_call(
        functools.partial(head_kernel, groups, chunks),
        in_specs=[VM] * 5,
        out_specs=[ANY] * 5,
        out_shape=[jax.ShapeDtypeStruct(tokens.shape, tokens.dtype)]
        + [jax.ShapeDtypeStruct(lead + s.shape, s.dtype) for lead, s in zip(shapes, shards)],
        scratch_shapes=[pltpu.SemaphoreType.DMA((slots,)), pltpu.SemaphoreType.DMA((slots,)), pltpu.SemaphoreType.DMA((5,))],
        compiler_params=pltpu.CompilerParams(collective_id=0, has_side_effects=True),
    )(tokens, *shards)


def tail_kernel(groups, tokens, own_lo, own_hi, rest_lo, rest_hi, small_lo, small_hi, x_out, total, vecs,
                part, got_core, got_near, got_last, got_far, vec, vec_core, vec_two, vec_one, vec_far, send_sem, recv_sem, local_sem):
    dp, t = lax.axis_index("dp"), lax.axis_index("tensor")
    core = dp % 2
    away = core + t - 2 * core * t
    near = {1: (flip(dp, (1,)), t), 2: (flip(dp, (2,)), t), 0: (dp, 1 - t)}
    distant = [bits for group in groups for _, bits in group_moves(group)]
    swap = (dp - core + t, core)
    barrier = pltpu.get_barrier_semaphore()
    for device in list(near.values()) + [(flip(dp, bits), t) for bits in distant]:
        pl.semaphore_signal(barrier, inc=1, device_id=device, device_id_type=MESH_ID)

    @pl.when(away == 1)
    def _():
        pl.semaphore_signal(barrier, inc=1, device_id=swap, device_id_type=MESH_ID)

    pl.semaphore_wait(barrier, len(near) + len(distant) + away)
    count = [0]

    def remote(src, dst, device):
        slot = count[0]
        count[0] += 1
        return pltpu.make_async_remote_copy(
            src_ref=src, dst_ref=dst, send_sem=send_sem.at[slot], recv_sem=recv_sem.at[slot],
            device_id=device, device_id_type=MESH_ID)

    swap_copy = remote(tokens, x_out, swap)
    stay_copy = pltpu.make_async_copy(tokens, x_out, local_sem.at[0])
    half, rows, cols = own_lo.shape
    cut = cols * 2 // 3 // 128 * 128
    a, b = pl.ds(0, cut), pl.ds(cut, cols - cut)
    quarter = half // 2
    to_core = [
        remote(rest_hi, got_core.at[0], near[1]), remote(own_hi, got_core.at[1], near[1]),
        remote(small_hi, vec_core, near[1])]
    for move in to_core:
        move.start()

    @pl.when(away == 1)
    def _():
        swap_copy.start()

    @pl.when(away == 0)
    def _():
        stay_copy.start()

    def add(*terms):
        out = terms[0].astype(f32)
        for term in terms[1:]:
            out = out + term.astype(f32)
        return out.astype(bf)

    for move in to_core:
        move.wait_recv()

    def sum_core(k, _):
        part[0, k] = add(own_lo[k], got_core[0, k])
        part[1, k] = add(rest_lo[k], got_core[1, k])
        vec[k] = add(small_lo[k], vec_core[k])
        return 0

    lax.fori_loop(0, half, sum_core, 0)
    upper, lower = pl.ds(quarter, quarter), pl.ds(0, quarter)
    mine, other = away, 1 - away
    to_near = [
        remote(part.at[0, upper, :, a], got_near.at[0, lower, :, a], near[2]),
        remote(part.at[1, upper, :, a], got_near.at[1, lower, :, a], near[2]),
        remote(part.at[other, :, :, b], got_near.at[0, :, :, b], near[0]),
        remote(vec.at[upper], vec_two, near[2])]
    for move in to_near:
        move.start()
    for move in to_near:
        move.wait_recv()

    def sum_near(k, _):
        for g in range(2):
            part[g, k, :, a] = add(part[g, k, :, a], got_near[g, k, :, a])
        for q in (k, k + quarter):
            part[mine, q, :, b] = add(part[mine, q, :, b], got_near[0, q, :, b])
        vec[k] = add(vec[k], vec_two[k])
        return 0

    lax.fori_loop(0, quarter, sum_near, 0)
    to_last = [
        remote(part.at[other, lower, :, a], got_last.at[:, :, a], near[0]),
        remote(part.at[mine, upper, :, b], got_last.at[:, :, b], near[2]),
        remote(vec.at[lower], vec_one, near[0])]
    for move in to_last:
        move.start()
    for move in to_last:
        move.wait_recv()

    def sum_last(k, _):
        part[mine, k] = add(part[mine, k], got_last[k])
        vec_one[k] = add(vec[k], vec_one[k])
        return 0

    lax.fori_loop(0, quarter, sum_last, 0)
    to_far = []
    held, used = quarter, 0
    for group in reversed(groups):
        moves = group_moves(group)
        held //= len(moves) + 1
        step = []
        for place, bits in moves:
            device = (flip(dp, bits), t)
            step.append(remote(part.at[mine, pl.ds(place * held, held)], got_far.at[pl.ds(used, held)], device))
            step.append(remote(vec_one.at[pl.ds(place * held, held)], vec_far.at[pl.ds(used, held)], device))
            used += held
        for move in step:
            move.start()
        for move in step:
            move.wait_recv()
        base = used - held * len(moves)

        def sum_far(k, _, base=base, held=held, count=len(moves)):
            part[mine, k] = add(part[mine, k], *[got_far[base + m * held + k] for m in range(count)])
            vec_one[k] = add(vec_one[k], *[vec_far[base + m * held + k] for m in range(count)])
            return 0

        lax.fori_loop(0, held, sum_far, 0)
        to_far += step
    total[...] = part[mine, 0].astype(f32)
    vecs[...] = vec_one[0].astype(f32)

    @pl.when(away == 1)
    def _():
        swap_copy.wait()

    @pl.when(away == 0)
    def _():
        stay_copy.wait()

    for move in to_core + to_near + to_last + to_far:
        move.wait_send()


def tail(dp_size, tokens, own, rest, small):
    groups = far_groups(dp_size)
    half, rows, cols = own[0].shape
    quarter = half // 2
    wide = small[0].shape[2]
    partners = sum(len(group_moves(g)) for g in groups)
    slots = 11 + 2 * partners
    return pl.pallas_call(
        functools.partial(tail_kernel, groups),
        in_specs=[VM] * 7,
        out_specs=[ANY, VM, VM],
        out_shape=[
            jax.ShapeDtypeStruct(tokens.shape, bf), jax.ShapeDtypeStruct((rows, cols), f32),
            jax.ShapeDtypeStruct((rows, wide), f32)],
        scratch_shapes=[
            pltpu.VMEM((2, half, rows, cols), bf), pltpu.VMEM((2, half, rows, cols), bf), pltpu.VMEM((2, half, rows, cols), bf),
            pltpu.VMEM((quarter, rows, cols), bf), pltpu.VMEM((quarter, rows, cols), bf),
            pltpu.VMEM((half, rows, wide), bf), pltpu.VMEM((half, rows, wide), bf), pltpu.VMEM((quarter, rows, wide), bf),
            pltpu.VMEM((quarter, rows, wide), bf), pltpu.VMEM((quarter, rows, wide), bf),
            pltpu.SemaphoreType.DMA((slots,)), pltpu.SemaphoreType.DMA((slots,)), pltpu.SemaphoreType.DMA((1,))],
        compiler_params=pltpu.CompilerParams(collective_id=1, has_side_effects=True, vmem_limit_bytes=48 << 20),
    )(tokens, *own, *rest, *small)


def far_exchange(value, dp_size):
    out, held = [], value.shape[0]
    (group,) = far_groups(dp_size)[-1:]
    held //= len(group_moves(group)) + 1
    for place, bits in group_moves(group):
        mask = sum(bits)
        piece = value[place * held : (place + 1) * held]
        out.append(lax.ppermute(piece, "dp", [(i, i ^ mask) for i in range(dp_size)]))
    return out


def far_sum(value, got, dp_size):
    held = got[0].shape[0]
    total = value[:held].astype(f32)
    for piece in got:
        total = total + piece.astype(f32)
    for group in far_groups(dp_size)[-2::-1]:
        total = total.astype(bf)
        held //= len(group_moves(group)) + 1
        moves = [
            lax.ppermute(total[place * held : (place + 1) * held], "dp", [(i, i ^ sum(bits)) for i in range(dp_size)])
            for place, bits in group_moves(group)]
        total = total[:held].astype(f32)
        for piece in moves:
            total = total + piece.astype(f32)
    return total


def add_low(*terms):
    out = terms[0].astype(f32)
    for term in terms[1:]:
        out = out + term.astype(f32)
    return out.astype(bf)


def order_matrix(owner, rows, width):
    place = lax.broadcasted_iota(jnp.int32, (1, width), 1)
    block = place // rows
    count = width // rows
    source = jnp.zeros_like(block)
    for k, bit in enumerate([1 << b for b in range(count.bit_length() - 2, 1, -1)] + [2, 1]):
        source = source + ((block // (1 << k)) % 2) * bit
    natural = (source ^ owner) * rows + place % rows
    return (lax.broadcasted_iota(jnp.int32, (width, width), 0) == natural).astype(f32).astype(bf)


def norm_parts(values):
    centered = values - jnp.mean(values, axis=-1, keepdims=True)
    inverse = lax.rsqrt(jnp.mean(centered * centered, axis=-1, keepdims=True) + EPSILON)
    return centered * inverse, inverse


def norm_back(hat, inverse, gain, grad):
    scaled = grad * gain
    return inverse * (
        scaled - jnp.mean(scaled, axis=-1, keepdims=True) - hat * jnp.mean(scaled * hat, axis=-1, keepdims=True))


def over_rows(total, body):
    def step(k, _):
        body(pl.ds(pl.multiple_of(k * ROWS, ROWS), ROWS))
        return 0

    lax.fori_loop(0, total // ROWS, step, 0)


def column_sum(ref, row, values):
    ref[row : row + 1] += jnp.sum(values, axis=0, keepdims=True)


def bias_row(vec_nat, group, cols):
    lanes = pl.ds(pl.multiple_of(group * cols, 128), cols)
    q, v = vec_nat[2:3, lanes], vec_nat[3:4, lanes]
    parts = []
    for g in range(cols // 128):
        part = slice(g * 128, (g + 1) * 128)
        parts += [q[:, part], jnp.zeros((1, 128), f32), v[:, part]]
    return jnp.concatenate(parts, axis=1)


def first_kernel(rows, info, tokens, pack, weight, x_out, n1_out, send, vec_rel, vec_nat, order):
    width, cols = tokens.shape[1], weight.shape[2] // 3
    order[...] = order_matrix(info[1], rows, width)
    small = pack[0, :, cols:].astype(f32).T[:VECS]
    vec_rel[...] = small
    vec_nat[...] = lax.dot_general(small.astype(bf), order[...], NT, preferred_element_type=f32)
    bias = bias_row(vec_nat, 1 - info[0], cols)

    def body(at):
        x = jnp.dot(tokens[at], order[...], preferred_element_type=f32)
        hat, _ = norm_parts(x)
        n1 = (hat * vec_rel[0:1] + vec_rel[1:2]).astype(bf)
        x_out[at] = x.astype(bf)
        n1_out[at] = n1
        send[at] = (jnp.dot(n1, weight[0], preferred_element_type=f32) + bias).astype(bf)

    over_rows(tokens.shape[0], body)


def own_kernel(info, n1, weight, vec_nat, out):
    bias = bias_row(vec_nat, info[0], weight.shape[2] // 3)

    def body(at):
        out[at] = (jnp.dot(n1[at], weight[0], preferred_element_type=f32) + bias).astype(bf)

    over_rows(n1.shape[0], body)


def picked(array, index):
    return pl.BlockSpec((1,) + array.shape[1:], lambda k, s: (index, 0, 0))


def whole(array):
    return pl.BlockSpec(array.shape, lambda k, s: (0,) * len(array.shape))


def one_call(kernel, info, inputs, specs, outs, scratch=(), limit=56):
    return pl.pallas_call(
        kernel,
        grid_spec=pltpu.PrefetchScalarGridSpec(
            num_scalar_prefetch=1, grid=(1,), in_specs=[s if s is not None else whole(a) for a, s in zip(inputs, specs)],
            out_specs=[whole(o) for o in outs], scratch_shapes=list(scratch)),
        out_shape=outs,
        cost_estimate=pl.CostEstimate(flops=1 << 22, bytes_accessed=1 << 18, transcendentals=0),
        compiler_params=pltpu.CompilerParams(vmem_limit_bytes=limit << 20),
    )(info, *inputs)


def like(shape, dtype):
    return jax.ShapeDtypeStruct(shape, dtype)


def project_first(info, rows, tokens, packs, weights):
    n, width = tokens.shape
    return one_call(
        functools.partial(first_kernel, rows), info, (tokens, packs, weights), (None, picked(packs, 0), picked(weights, 1)),
        [like((n, width), bf), like((n, width), bf), like((n, weights.shape[2]), bf), like((VECS, width), f32), like((VECS, width), f32)],
        [pltpu.VMEM((width, width), bf)])


def project_own(info, n1, weights, vec_nat):
    (out,) = one_call(
        own_kernel, info, (n1, weights, vec_nat), (None, picked(weights, 0), None), [like((n1.shape[0], weights.shape[2]), bf)])
    return out


def feed_kernel(rows, info, o_own, o_recv, packs, x, vec_rel, cot, cot_recv, bias, fc00, fc01, fc02, fc03, fc10, fc11, fc12, fc13,
                pr00, pr01, pr10, pr11, block_out, d_middle, d_attn, do_own, do_send, sums, fc_lo, fc_hi, pr_lo, pr_hi, d_bias,
                order, n2, d_mlp, n2_t, d_t, w_fc, w_pr, act, d_pre, acc, back):
    step = pl.program_id(0)
    width, cols = x.shape[1], o_own.shape[1]
    total, half = x.shape[0], width // 2

    @pl.when(step == 0)
    def _():
        order[...] = order_matrix(info[1], rows, width)
        stay = info[2] == 1
        acc[...] = jnp.zeros_like(acc)
        back[...] = jnp.zeros_like(back)

        def body(at):
            branch = lax.dot_general(o_own[at], packs[0, :, :cols], NT, preferred_element_type=f32)
            branch = branch + lax.dot_general(o_recv[at], packs[1, :, :cols], NT, preferred_element_type=f32)
            mid = x[at].astype(f32) + BRANCH_SCALE * (branch + vec_rel[4:5])
            d_middle[at] = mid
            hat, _ = norm_parts(mid)
            n2[at] = (hat * vec_rel[5:6] + vec_rel[6:7]).astype(bf)
            grad = jnp.dot(jnp.where(stay, cot[at], cot_recv[at]), order[...], preferred_element_type=f32)
            d_attn[at] = grad.astype(bf)
            d_mlp[at] = (BRANCH_SCALE * grad).astype(bf)

        over_rows(total, body)
        n2_t[...] = n2[...].T
        d_t[...] = d_mlp[...].T

    def load(target, pieces):
        at = 0
        for piece in pieces:
            target[at : at + piece.shape[0]] = piece[...]
            at += piece.shape[0]

    @pl.when(step < pl.num_programs(0) // 2)
    def _():
        load(w_fc, (fc00, fc01, fc02, fc03))
        load(w_pr, (pr00, pr01))

    @pl.when(step >= pl.num_programs(0) // 2)
    def _():
        load(w_fc, (fc10, fc11, fc12, fc13))
        load(w_pr, (pr10, pr11))

    root = 0.7978845608
    count = total // ROWS
    raw = {}
    grad_sum = jnp.zeros((1, w_fc.shape[1]), f32)

    def products(k):
        at = slice(k * ROWS, (k + 1) * ROWS)
        return (
            jnp.dot(n2[at], w_fc[...], preferred_element_type=f32) + bias[0],
            jnp.dot(d_mlp[at], w_pr[...], preferred_element_type=f32))

    raw[0] = products(0)
    for k in range(count):
        at = slice(k * ROWS, (k + 1) * ROWS)
        if k + 1 < count:
            raw[k + 1] = products(k + 1)
        pre, d_act = raw.pop(k)
        square = pre * pre
        inner = jnp.tanh(pre * (root + root * 0.044715 * square))
        gate = 0.5 + 0.5 * inner
        act[at] = (pre * gate).astype(bf)
        slope = gate + pre * (0.5 - 0.5 * inner * inner) * (root + root * 3 * 0.044715 * square)
        grad = d_act * slope
        grad_sum = grad_sum + jnp.sum(grad, axis=0, keepdims=True)
        d_pre[at] = grad.astype(bf)
        if k > 0:
            add_back(k - 1, acc, back, act, d_pre, w_pr, w_fc)
    add_back(count - 1, acc, back, act, d_pre, w_pr, w_fc)
    d_bias[0] = grad_sum
    for out, left, right, low in (
        (fc_hi, n2_t, d_pre, half), (pr_hi, d_t, act, half), (fc_lo, n2_t, d_pre, 0), (pr_lo, d_t, act, 0)):
        out[0] = jnp.dot(left[low : low + half], right[...], preferred_element_type=f32).astype(bf)

    @pl.when(step == pl.num_programs(0) - 1)
    def _():
        sums[...] = jnp.zeros_like(sums)

        def body(at):
            mid = d_middle[at]
            out = (mid + BRANCH_SCALE * (acc[at] + vec_rel[7:8])).astype(bf)
            block_out[at] = lax.dot_general(out, order[...], NT, preferred_element_type=f32).astype(bf)
            hat, inverse = norm_parts(mid)
            grad = back[at]
            out_grad = d_attn[at].astype(f32)
            entire = out_grad + norm_back(hat, inverse, vec_rel[5:6], grad)
            d_middle[at] = entire
            low = (BRANCH_SCALE * entire).astype(bf)
            d_attn[at] = low
            do_own[at] = jnp.dot(low, packs[0, :, :cols], preferred_element_type=f32).astype(bf)
            do_send[at] = jnp.dot(low, packs[1, :, :cols], preferred_element_type=f32).astype(bf)
            column_sum(sums, 0, BRANCH_SCALE * entire)
            column_sum(sums, 1, grad * hat)
            column_sum(sums, 2, grad)
            column_sum(sums, 3, BRANCH_SCALE * out_grad)

        over_rows(total, body)


def add_back(k, acc, back, act, d_pre, w_pr, w_fc):
    at = slice(k * ROWS, (k + 1) * ROWS)
    acc[at] += lax.dot_general(act[at], w_pr[...], NT, preferred_element_type=f32)
    back[at] += lax.dot_general(d_pre[at], w_fc[...], NT, preferred_element_type=f32)


def feed_part(info, rows, o_own, o_recv, packs, x, vec_rel, cot, cot_recv, bias, fc_parts, proj_parts):
    (total, width), cols = x.shape, o_own.shape[1]
    hidden, half = bias.shape[2], width // 2
    steps = hidden // HIDDEN
    fixed = lambda a: pl.BlockSpec(a.shape, lambda k, s: (0,) * len(a.shape), pipeline_mode=pl.Buffered(1))
    early = lambda a: pl.BlockSpec((a.shape[0], HIDDEN), lambda k, s: (0, jnp.minimum(k, steps - 1)))
    late = lambda a: pl.BlockSpec((a.shape[0], HIDDEN), lambda k, s: (0, jnp.maximum(k - steps, 0)))
    two = lambda a: pl.BlockSpec((1, a.shape[1], HIDDEN), lambda k, s: (k // steps, 0, k % steps))
    firsts = (o_own, o_recv, packs, x, vec_rel, cot, cot_recv)
    grad = like((2, half, hidden), bf)
    slim = like((total, cols), bf)
    plain = [like((total, width), bf), like((total, width), f32), like((total, width), bf), slim, slim, like((8, width), f32)]
    outs = plain + [grad] * 4 + [like((2, 1, hidden), f32)]
    return pl.pallas_call(
        functools.partial(feed_kernel, rows),
        grid_spec=pltpu.PrefetchScalarGridSpec(
            num_scalar_prefetch=1,
            grid=(2 * steps,),
            in_specs=[fixed(a) for a in firsts] + [two(bias)]
            + [early(a) for a in fc_parts[0]] + [late(a) for a in fc_parts[1]]
            + [early(a) for a in proj_parts[0]] + [late(a) for a in proj_parts[1]],
            out_specs=[fixed(o) for o in plain] + [two(o) for o in outs[len(plain) :]],
            scratch_shapes=[
                pltpu.VMEM((width, width), bf), pltpu.VMEM((total, width), bf), pltpu.VMEM((total, width), bf),
                pltpu.VMEM((width, total), bf), pltpu.VMEM((width, total), bf), pltpu.VMEM((width, HIDDEN), bf),
                pltpu.VMEM((width, HIDDEN), bf), pltpu.VMEM((total, HIDDEN), bf), pltpu.VMEM((total, HIDDEN), bf),
                pltpu.VMEM((total, width), f32), pltpu.VMEM((total, width), f32)],
        ),
        out_shape=outs,
        cost_estimate=pl.CostEstimate(flops=1 << 22, bytes_accessed=1 << 18, transcendentals=0),
        compiler_params=pltpu.CompilerParams(vmem_limit_bytes=60 << 20),
    )(info, *firsts, bias, *fc_parts[0], *fc_parts[1], *proj_parts[0], *proj_parts[1])


def grads_into(lo, hi, left_t, extra_t, d_qkv, o):
    half = left_t.shape[0] // 2
    wide = d_qkv.shape[1]
    for out, low in ((hi, half), (lo, 0)):
        out[:, :wide] = jnp.dot(left_t[low : low + half], d_qkv[...], preferred_element_type=f32).astype(bf)
        out[:, wide:] = jnp.dot(extra_t[low : low + half], o[...], preferred_element_type=f32).astype(bf)


def last_own_kernel(info, d_qkv, n1, d_attn, o_own, weight, lo, hi, part, sums, left_t, extra_t):
    left_t[...] = n1[...].T
    extra_t[...] = d_attn[...].T
    sums[...] = jnp.zeros_like(sums)
    grads_into(lo, hi, left_t, extra_t, d_qkv, o_own)

    def body(at):
        part[at] = lax.dot_general(d_qkv[at], weight[0], NT, preferred_element_type=f32)
        column_sum(sums, 0, d_qkv[at].astype(f32))

    over_rows(n1.shape[0], body)


def last_own(info, dq, n1, d_attn, o_own, weights):
    n, width = n1.shape
    wide, slim = weights.shape[2], o_own.shape[1]
    grad = like((width // 2, wide + slim), bf)
    return one_call(
        last_own_kernel, info, (dq, n1, d_attn, o_own, weights), (None,) * 4 + (picked(weights, 0),),
        [grad, grad, like((n, width), f32), like((8, wide), f32)],
        [pltpu.VMEM((width, n), bf), pltpu.VMEM((width, n), bf)])


def last_kernel(rows, info, d_qkv, n1, d_attn, o_recv, weight, part, x, d_middle, vec_rel, own_sums, mid_sums, fc_rows,
                lo, hi, grad_out, small, left_t, extra_t, sums, vecs, nat, order):
    width, cols = x.shape[1], o_recv.shape[1]
    order[...] = order_matrix(info[1], rows, width)
    left_t[...] = n1[...].T
    extra_t[...] = d_attn[...].T
    sums[...] = jnp.zeros_like(sums)
    vecs[...] = jnp.zeros_like(vecs)
    grads_into(lo, hi, left_t, extra_t, d_qkv, o_recv)

    def body(at):
        grad = part[at] + lax.dot_general(d_qkv[at], weight[0], NT, preferred_element_type=f32)
        hat, inverse = norm_parts(x[at].astype(f32))
        grad_out[at] = (d_middle[at] + norm_back(hat, inverse, vec_rel[0:1], grad)).astype(bf)
        column_sum(sums, 0, d_qkv[at].astype(f32))
        column_sum(vecs, 0, grad * hat)
        column_sum(vecs, 1, grad)

    over_rows(x.shape[0], body)
    nat[...] = jnp.zeros_like(nat)
    for group, ref in ((info[0], own_sums), (1 - info[0], sums)):
        for row, part_index in ((0, 0), (1, 2)):
            picks = [ref[0:1, (3 * g + part_index) * 128 : (3 * g + part_index + 1) * 128] for g in range(cols // 128)]
            nat[row : row + 1, pl.ds(pl.multiple_of(group * cols, 128), cols)] = jnp.concatenate(picks, axis=1)
    fan = fc_rows.shape[0]
    nat[2 : 2 + fan] = fc_rows[...]
    moved = jnp.dot(nat[...].astype(bf), order[...], preferred_element_type=f32)
    vecs[2:4] = moved[0:2]
    vecs[4:8] = mid_sums[0:4]
    vecs[8 : 8 + fan] = moved[2 : 2 + fan]
    small[...] = vecs[...].T.astype(bf)


def last_part(info, rows, dq, n1, d_attn, o_recv, weights, part, x, d_middle, vec_rel, own_sums, mid_sums, fc_rows):
    n, width = n1.shape
    wide, slim = weights.shape[2], o_recv.shape[1]
    grad = like((width // 2, wide + slim), bf)
    inputs = (dq, n1, d_attn, o_recv, weights, part, x, d_middle, vec_rel, own_sums, mid_sums, fc_rows)
    return one_call(
        functools.partial(last_kernel, rows), info, inputs, (None,) * 4 + (picked(weights, 1),) + (None,) * 7,
        [grad, grad, like((n, width), bf), like((width, SMALL), bf)],
        [pltpu.VMEM((width, n), bf), pltpu.VMEM((width, n), bf), pltpu.VMEM((8, wide), f32),
         pltpu.VMEM((SMALL, width), f32), pltpu.VMEM((8, width), f32), pltpu.VMEM((width, width), bf)])


def on_device(
    tokens, segment_ids, ln1_gain, ln1_bias, w_qkv, b_qv, w_attn_out, b_attn_out,
    ln2_gain, ln2_bias, w_fc, b_fc, w_proj, b_proj, cotangent,
):
    dp_size = lax.axis_size("dp")
    dp_pos, t_pos = lax.axis_index("dp"), lax.axis_index("tensor")
    core = dp_pos % 2
    rows = ln1_gain.shape[0]
    width = tokens.shape[1]
    cols = w_qkv.shape[2]
    hidden = w_fc.shape[1]
    fan = b_fc.shape[0] // rows
    far = [1 << k for k in range(dp_size.bit_length() - 2, 1, -1)]
    swap = []
    for d in range(dp_size):
        for t in range(2):
            if d % 2 != t:
                swap.append((2 * d + t, 2 * (d - d % 2 + t) + d % 2))
    mine = core == t_pos

    pairs = cols // 128

    def by_pair(parts):
        parts = parts.reshape(-1, 3, pairs, 128)
        return jnp.swapaxes(parts, 1, 2).reshape(-1, 3 * cols)

    def by_part(columns):
        return jnp.swapaxes(columns.reshape(-1, pairs, 3, 128), 1, 2).reshape(-1, 3, cols)

    seg_other = exchange(segment_ids, 1, dp_size)
    seg = jnp.where(mine, segment_ids, seg_other)[0]
    small = jnp.concatenate(
        [ln1_gain[:, None], ln1_bias[:, None], b_qv.T, b_attn_out[:, None], ln2_gain[:, None],
         ln2_bias[:, None], b_proj[:, None], b_fc.reshape(rows, fan)], axis=1)
    small = jnp.pad(small, ((0, 0), (0, SMALL - small.shape[1])))
    out_pack = jnp.concatenate([w_attn_out.T, small], axis=1)
    tokens, all_qkv, all_out, fc_far, proj_far = head(
        dp_size, tokens, (by_pair(w_qkv), out_pack, w_fc, w_proj.T), chunks_of(3 * cols, 0, 2) + chunks_of(cols + SMALL, 1, 1))
    all_qkv, all_out = (a.reshape(2, width, -1) for a in (all_qkv, all_out))
    fc_far, proj_far = fc_far.reshape(-1, hidden), proj_far.reshape(-1, hidden)
    fc_parts = [[fc_far], [exchange(fc_far, 0, dp_size)]]
    proj_half = exchange(proj_far, 2, dp_size)

    part = jnp.stack([core, dp_pos, jnp.where(mine, 1, 0)]).astype(jnp.int32)
    x, n1, qkv_send, vec_rel, vec_nat = project_first(part, rows, tokens, all_out, all_qkv)
    qkv_recv = exchange(qkv_send, 1, dp_size)
    fc_parts, proj_half, n1 = lax.optimization_barrier((fc_parts, proj_half, n1))
    fc_parts = [p + [exchange(p[0], 2, dp_size)] for p in fc_parts]
    proj_half = jnp.concatenate([proj_far, proj_half], axis=0)
    proj_parts = [[proj_half], [exchange(proj_half, 0, dp_size)]]
    qkv_own = project_own(part, n1, all_qkv, vec_nat)
    starts, info = attn_info(seg, core)
    o_own, o_send, lse = attn_fwd(qkv_own, qkv_recv, starts, info)
    fc_parts, proj_parts, o_own, o_send = lax.optimization_barrier((fc_parts, proj_parts, o_own, o_send))
    o_recv = exchange(o_send, 1, dp_size)
    fc_parts, proj_parts = (
        [p + [exchange(e, 1, dp_size) for e in p] for p in parts] for parts in (fc_parts, proj_parts))
    cot_recv = lax.ppermute(cotangent, BOTH, swap)
    fc_bias = vec_nat[8 : 8 + fan].T.reshape(2, 1, hidden)
    fc_bias = jnp.where(t_pos == 0, fc_bias, fc_bias[::-1])
    half = width // 2
    (block_out, d_middle, d_attn, do_own, do_send, mid_sums, fc_lo, fc_hi, pr_lo, pr_hi, d_b_fc) = feed_part(
        part, rows, o_own, o_recv, all_out, x, vec_rel, cotangent, cot_recv, fc_bias, fc_parts, proj_parts)
    do_recv = exchange(do_send, 1, dp_size)
    fc_got, pr_got = exchange(fc_hi, 1, dp_size), exchange(pr_hi, 1, dp_size)
    fc_rows = jnp.where(t_pos == 0, d_b_fc, d_b_fc[::-1]).reshape(width, fan).T

    near_size = half // 2
    fc_rest = add_low(fc_lo[1], fc_got[1])
    pr_rest = add_low(pr_lo[:, near_size:], pr_got[:, near_size:])
    last = (qkv_own, qkv_recv, do_own, do_recv, o_own, o_send)
    last, fc_rest, pr_rest = lax.optimization_barrier((last, fc_rest, pr_rest))
    fc_sent = exchange(fc_rest, 0, dp_size)
    pr_sent = exchange(pr_rest, 2, dp_size)
    dq_own, dq_send = attn_bwd(*last, starts, lse, info)
    dq_recv = exchange(dq_send, 1, dp_size)
    dq_own, fc_sent, pr_sent, block_out = lax.optimization_barrier((dq_own, fc_sent, pr_sent, block_out))
    fc_rest = add_low(fc_lo[0, near_size:], fc_got[0, near_size:], fc_sent[near_size:])
    pr_rest = add_low(pr_lo[1, :near_size], pr_got[1, :near_size], pr_sent[1])
    dq_own, fc_rest, pr_rest = lax.optimization_barrier((dq_own, fc_rest, pr_rest))
    fc_near = exchange(fc_rest, 2, dp_size)
    pr_near = exchange(pr_rest, 0, dp_size)
    own_lo, own_hi, d_n1, own_sums = last_own(part, dq_own, n1, d_attn, o_own, all_qkv)
    d_n1, fc_near, pr_near = lax.optimization_barrier((d_n1, fc_near, pr_near))
    sum_fc = add_low(fc_lo[0, :near_size], fc_got[0, :near_size], fc_sent[:near_size], fc_near)
    sum_proj = add_low(pr_lo[0, :near_size], pr_got[0, :near_size], pr_sent[0], pr_near)
    d_n1, sum_fc, sum_proj, block_out = lax.optimization_barrier((d_n1, sum_fc, sum_proj, block_out))
    block_recv = lax.ppermute(block_out, BOTH, swap)
    fc_sent = far_exchange(sum_fc, dp_size)
    proj_sent = far_exchange(sum_proj, dp_size)
    own_lo, own_hi, d_n1, own_sums = last_own(part, dq_own, n1, d_attn, o_own, all_qkv)
    rest_lo, rest_hi, grad_tokens, d_small = last_part(
        part, rows, dq_recv, n1, d_attn, o_recv, all_qkv, d_n1, x, d_middle, vec_rel, own_sums, mid_sums, fc_rows)
    blocks = lambda arr: arr.reshape(dp_size // 2, rows, -1)
    grad_tokens, sum_a, vecs = tail(
        dp_size, grad_tokens, (blocks(own_lo), blocks(own_hi)), (blocks(rest_lo), blocks(rest_hi)),
        (blocks(d_small[:half]), blocks(d_small[half:])))
    vecs, fc_sent, proj_sent, block_recv = lax.optimization_barrier((vecs, fc_sent, proj_sent, block_recv))
    block_out = jnp.where(mine, block_out, block_recv)
    owner = dp_pos - core + t_pos
    grad_tokens = dot(grad_tokens, order_matrix(owner, rows, width), NT).astype(bf)
    sum_fc, sum_proj = far_sum(sum_fc, fc_sent, dp_size), far_sum(sum_proj, proj_sent, dp_size)
    return (
        block_out,
        grad_tokens,
        vecs[:, 0],
        vecs[:, 1],
        by_part(sum_a[:, : 3 * cols]),
        vecs[:, 2:4].T,
        sum_a[:, 3 * cols :].T,
        vecs[:, 4],
        vecs[:, 5],
        vecs[:, 6],
        sum_fc.astype(f32),
        vecs[:, 8 : 8 + fan].reshape(rows * fan),
        sum_proj.astype(f32).T,
        vecs[:, 7],
    )


def solution(mesh):
    vec, tok = P("dp"), P(BOTH, None)
    in_specs = (
        tok, P("dp", None), vec, vec, P("dp", None, "tensor"), P(None, "dp"), P("tensor", "dp"),
        vec, vec, vec, P("dp", "tensor"), vec, P("tensor", "dp"), vec, tok,
    )
    out_specs = (
        tok, tok, vec, vec, P("dp", None, "tensor"), P(None, "dp"), P("tensor", "dp"),
        vec, vec, vec, P("dp", "tensor"), vec, P("tensor", "dp"), vec,
    )
    return jax.shard_map(on_device, mesh=mesh, in_specs=in_specs, out_specs=out_specs, check_vma=False)
```

profile of v0, /device:TPU:0, one launch (start us, length us, event | category | flops | bytes accessed | tf_op | source)
XLA Modules:
  0.0 387.9 jit_solution(14247406641406682774)
XLA Ops:
  10.6 57.9 %shard_map.254 = (bf16[1024,768]{1,0:T(8,128)(2,1)}, bf16[2,16,48,1152]{3,2,1,0:T(8,128)(2,1)}, bf16[2,16,48,512]{3,2,1,0:T(8,128)(2,1)}, bf16[4,48,1536]{2,1,0:T(8,128)(2,1)}, bf16[4,48,1536]{2,1,0:T(8,128)(2,1)}) custom-call(bf16[1024,768]{1,0:T(8,128)(2,1)} %tokens.1, bf16[48,1152]{1,0:T(8,128)(2,1)} %reshape.332.refs_0_, bf16[48,512]{1,0:T(8,128)(2,1)} %fusion.8.refs_1_, ...), custom_call_target="tpu_custom_call" | custom-call | tf_op jit(solution)/shard_map/pallas_call | solution.py:385
  68.5 11.3 %shard_map.255 = (bf16[1024,768]{1,0:T(8,128)(2,1)}, bf16[1024,768]{1,0:T(8,128)(2,1)}, bf16[1024,1152]{1,0:T(8,128)(2,1)}, f32[16,768]{1,0:T(8,128)}, f32[16,768]{1,0:T(8,128)}) custom-call(s32[3]{0:T(128)} %pad_add_fusion.info, bf16[1024,768]{1,0:T(8,128)(2,1)} %get-tuple-element.93.tokens, bf16[2,768,512]{2,1,0:T(8,128)(2,1)} %bitcast.70, ...), custom_call_target="tpu_custom_call" | custom-call | flops 4194304 | bytes 262144 | tf_op jit(solution)/shard_map/pallas_call | solution.py:674
  80.8 15.0 %collective-permute-done.fc10 = bf16[192,1536]{1,0:T(8,128)(2,1)} collective-permute-done((bf16[192,1536]{1,0:T(8,128)(2,1)}, bf16[192,1536]{1,0:T(8,128)(2,1)}, u32[]{:S(2)}, u32[]{:S(2)}) %collective-permute-start) | collective-permute-done | bytes 589856 | tf_op jit(solution)/shard_map/ppermute | solution.py:219
  98.4 1.8 collective-permute-start.8
  102.8 6.8 %shard_map.256.own = bf16[1024,1152]{1,0:T(8,128)(2,1)} custom-call(s32[3]{0:T(128)} %pad_add_fusion.info, bf16[1024,768]{1,0:T(8,128)(2,1)} %get-tuple-element.100.n1, bf16[2,768,1152]{2,1,0:T(8,128)(2,1)} %bitcast.67, f32[16,768]{1,0:T(8,128)} %get-tuple-element.101.vec_nat), custom_call_target="tpu_custom_call" | custom-call | flops 4194304 | bytes 262144 | tf_op jit(solution)/shard_map/pallas_call | solution.py:674
  111.0 1.7 copy-done
  112.7 21.5 %shard_map.257 = (bf16[1024,384]{1,0:T(8,128)(2,1)S(1)}, bf16[1024,384]{1,0:T(8,128)(2,1)S(1)}, f32[6,2048]{1,0:T(8,128)S(1)}) custom-call(s32[17]{0:T(128)S(1)} %pad_add_fusion.1.info, bf16[1024,1152]{1,0:T(8,128)(2,1)S(1)} %copy-done, bf16[1024,1152]{1,0:T(8,128)(2,1)} %copy-done.10, s32[1,2048]{1,0:T(1,128)S(1)} %bitcast.64), custom_call_target="tpu_custom_call" | custom-call | flops 4194304 | bytes 262144 | tf_op jit(solution)/shard_map/pallas_call | solution.py:114
  136.8 4.6 %collective-permute-start.7 = (bf16[1024,384]{1,0:T(8,128)(2,1)S(1)}, bf16[1024,384]{1,0:T(8,128)(2,1)S(1)}, u32[]{:S(2)}, u32[]{:S(2)}) collective-permute-start(bf16[1024,384]{1,0:T(8,128)(2,1)S(1)} %get-tuple-element.126.orr), channel_id=1, source_target_pairs={{0,2},{2,0},{4,6},{6,4},{8,10},{10,8},{12,14},{14,12},{16,18},{18,... | collective-permute-start | bytes 2359304 | tf_op jit(solution)/shard_map/ppermute | solution.py:218
  146.7 54.7 %shard_map.258 = (bf16[1024,768]{1,0:T(8,128)(2,1)}, f32[1024,768]{1,0:T(8,128)}, bf16[1024,768]{1,0:T(8,128)(2,1)}, bf16[1024,384]{1,0:T(8,128)(2,1)}, bf16[102...) custom-call(s32[3]{0:T(128)} %pad_add_fusion.info, ...), custom_call_target="tpu_custom_call" | custom-call | flops 4194304 | bytes 262144 | tf_op jit(solution)/shard_map/pallas_call | solution.py:825
  202.4 3.9 collective-permute-done.17
  206.2 3.5 add_convert_fusion
  209.7 1.5 fusion
  211.6 2.0 collective-permute-start.18
  214.5 33.1 %shard_map.259 = (bf16[1024,1152]{1,0:T(8,128)(2,1)}, bf16[1024,1152]{1,0:T(8,128)(2,1)}) custom-call(s32[17]{0:T(128)} %copy-done.9, bf16[1024,1152]{1,0:T(8,128)(2,1)} %shard_map.256.own, bf16[1024,1152]{1,0:T(8,128)(2,1)} %copy-done.10, bf16[1024,384]{1,0:T(8,128)(2,1)} %get-tuple-element.123.doo, bf16[1024,384]{1,0:T(8,128)(2,1)} %copy-done.19, ...), custom_call_target="tpu_custom_call" | custom-call | flops 4194304 | bytes 262144 | tf_op jit(solution)/shard_map/pallas_call | solution.py:198
  247.6 2.5 fusion.6
  250.1 2.1 fusion.2
  254.7 12.1 %shard_map.260 = (bf16[384,1536]{1,0:T(8,128)(2,1)}, bf16[384,1536]{1,0:T(8,128)(2,1)}, f32[1024,768]{1,0:T(8,128)}, f32[8,1152]{1,0:T(8,128)}) custom-call(s32[3]{0:T(128)} %pad_add_fusion.info, bf16[1024,1152]{1,0:T(8,128)(2,1)} %get-tuple-element.135.d_qkv, bf16[1024,768]{1,0:T(8,128)(2,1)} %get-tuple-element.100.n1, ...), custom_call_target="tpu_custom_call" | custom-call | flops 4194304 | bytes 262144 | tf_op jit(solution)/shard_map/pallas_call | solution.py:674
  266.8 1.5 collective-permute-done.20
  269.9 2.5 fusion.1
  274.0 7.1 %collective-permute-start.23 = (bf16[48,1536]{1,0:T(8,128)(2,1)}, bf16[48,1536]{1,0:T(8,128)(2,1)S(1)}, u32[]{:S(2)}, u32[]{:S(2)}) collective-permute-start(bf16[48,1536]{1,0:T(8,128)(2,1)} %get-tuple-element.253), channel_id=1, source_target_pairs={{0,16},{2,18},{4,20},{6,22},{8,24},{10,26},{12,28},{14,30},{16,0},... | collective-permute-start | bytes 442376 | tf_op jit(solution)/shard_map/ppermute | solution.py:564
  281.0 1.5 collective-permute-start.25
  283.3 2.0 collective-permute-start.26
  285.3 15.6 %shard_map.261 = (bf16[384,1536]{1,0:T(8,128)(2,1)}, bf16[384,1536]{1,0:T(8,128)(2,1)}, bf16[1024,768]{1,0:T(8,128)(2,1)}, bf16[768,128]{1,0:T(8,128)(2,1)}) custom-call(s32[3]{0:T(128)} %pad_add_fusion.info, bf16[1024,1152]{1,0:T(8,128)(2,1)} %collective-permute-done.22.d_qkv, bf16[1024,768]{1,0:T(8,128)(2,1)} %get-tuple-element.100.n1, ...), custom_call_target="tpu_custom_call" | custom-call | flops 4194304 | bytes 262144 | tf_op jit(solution)/shard_map/pallas_call | solution.py:674
  304.5 55.5 %shard_map.262 = (bf16[1024,768]{1,0:T(8,128)(2,1)}, f32[48,1536]{1,0:T(8,128)S(1)}, f32[48,128]{1,0:T(8,128)S(1)}) custom-call(bf16[1024,768]{1,0:T(8,128)(2,1)} %get-tuple-element.149.tokens, bf16[8,48,1536]{2,1,0:T(8,128)(2,1)S(1)} %bitcast.58, bf16[8,48,1536]{2,1,0:T(8,128)(2,1)S(1)} %bitcast.59, bf16[8,48,1536]{2,1,0:T(8,128)(2,1)S(1)} %bitcast.60, ...), custom_call_target="tpu_custom_call" | custom-call | tf_op jit(solution)/shard_map/pallas_call | solution.py:540
  360.0 4.0 %convolution_convert_fusion = bf16[1024,768]{1,0:T(8,128)(2,1)} fusion(bf16[1024,768]{1,0:T(8,128)(2,1)} %get-tuple-element.159, s32[768]{0:T(1024)S(1)} %fusion.22), kind=kOutput, calls=%fused_computation.4 | convolution fusion | flops 1210515456 | bytes 3148800 | tf_op jit(solution)/shard_map/dot_general | solution.py:213
  366.5 1.8 reshape.349
  368.3 2.9 collective-permute-start.27
  372.2 3.6 collective-permute-done.27
  375.8 3.2 collective-permute-done.28
  379.9 2.7 broadcast_select_fusion
  383.9 1.7 add_bitcast_fusion
  385.6 1.8 convert_add_fusion
  (137 shorter events, 43.0 us)
Async XLA Ops:
  79.8 29.8 %collective-permute-start.6 = (bf16[1024,1152]{1,0:T(8,128)(2,1)}, bf16[1024,1152]{1,0:T(8,128)(2,1)S(1)}, u32[]{:S(2)}, u32[]{:S(2)}) collective-permute-start(bf16[1024,1152]{1,0:T(8,128)(2,1)} %get-tuple-element.102), channel_id=1, source_target_pairs={{0,2},{2,0},{4,6},{6,4},{8,10},{10,8},{12,14},{14,12},{16,18},{18,... | collective-permute-start | bytes 7077896 | tf_op jit(solution)/shard_map/ppermute | solution.py:218
  79.8 16.0 %collective-permute-start = (bf16[192,1536]{1,0:T(8,128)(2,1)}, bf16[192,1536]{1,0:T(8,128)(2,1)}, u32[]{:S(2)}, u32[]{:S(2)}) collective-permute-start(bf16[192,1536]{1,0:T(8,128)(2,1)} %bitcast.13.fc00), channel_id=1, source_target_pairs={{0,1},{1,0},{2,3},{3,2},{4,5},{5,4},{6,7},{7,6},{8,9},{9,8},{10,11... | collective-permute-start | bytes 1769480 | tf_op jit(solution)/shard_map/ppermute | solution.py:219
  79.9 16.0 %collective-permute-start.1 = (bf16[192,1536]{1,0:T(8,128)(2,1)S(1)}, bf16[192,1536]{1,0:T(8,128)(2,1)S(1)}, u32[]{:S(2)}, u32[]{:S(2)}) collective-permute-start(bf16[192,1536]{1,0:T(8,128)(2,1)S(1)} %bitcast.74), channel_id=1, source_target_pairs={{0,4},{2,6},{4,0},{6,2},{8,12},{10,14},{12,8},{14,10},{16,20},{18,... | collective-permute-start | bytes 1769480 | tf_op jit(solution)/shard_map/ppermute | solution.py:218
  97.0 38.8 %collective-permute-start.4 = (bf16[384,1536]{1,0:T(8,128)(2,1)}, bf16[384,1536]{1,0:T(8,128)(2,1)}, u32[]{:S(2)}, u32[]{:S(2)}) collective-permute-start(bf16[384,1536]{1,0:T(8,128)(2,1)} %pad_maximum_fusion.pr00), channel_id=1, source_target_pairs={{0,1},{1,0},{2,3},{3,2},{4,5},{5,4},{6,7},{7,6},{8,9},{9,8},{10,11... | collective-permute-start | bytes 3538952 | tf_op jit(solution)/shard_map/ppermute | solution.py:219
  98.4 1.8 collective-permute-start.5
  98.4 38.4 %collective-permute-start.8 = (bf16[1024,768]{1,0:T(8,128)(2,1)}, bf16[1024,768]{1,0:T(8,128)(2,1)}, u32[]{:S(2)}, u32[]{:S(2)}) collective-permute-start(bf16[1024,768]{1,0:T(8,128)(2,1)} %cot.1), channel_id=1, source_target_pairs={{1,2},{2,1},{5,6},{6,5},{9,10},{10,9},{13,14},{14,13},{17,18},{18,... | collective-permute-start | bytes 4718600 | tf_op jit(solution)/shard_map/ppermute | solution.py:979
  100.2 35.5 %collective-permute-start.2 = (bf16[192,1536]{1,0:T(8,128)(2,1)}, bf16[192,1536]{1,0:T(8,128)(2,1)}, u32[]{:S(2)}, u32[]{:S(2)}) collective-permute-start(bf16[192,1536]{1,0:T(8,128)(2,1)} %bitcast.13.fc00), channel_id=1, source_target_pairs={{0,4},{2,6},{4,0},{6,2},{8,12},{10,14},{12,8},{14,10},{16,20},{18,... | collective-permute-start | bytes 1769480 | tf_op jit(solution)/shard_map/ppermute | solution.py:218
  101.2 34.6 %collective-permute-start.3 = (bf16[192,1536]{1,0:T(8,128)(2,1)}, bf16[192,1536]{1,0:T(8,128)(2,1)}, u32[]{:S(2)}, u32[]{:S(2)}) collective-permute-start(bf16[192,1536]{1,0:T(8,128)(2,1)} %collective-permute-done.fc10), channel_id=1, source_target_pairs={{0,4},{2,6},{4,0},{6,2},{8,12},{10,14},{12,8},{14,10},{16,20},{18,... | collective-permute-start | bytes 1769480 | tf_op jit(solution)/shard_map/ppermute | solution.py:218
  135.7 65.7 %copy-start.6 = (bf16[1024,384]{1,0:T(8,128)(2,1)}, bf16[1024,384]{1,0:T(8,128)(2,1)S(1)}, u32[]{:S(2)}) copy-start(bf16[1024,384]{1,0:T(8,128)(2,1)S(1)} %get-tuple-element.126.orr) | copy-start | bytes 2359300
  135.7 5.7 %collective-permute-start.10 = (bf16[192,1536]{1,0:T(8,128)(2,1)}, bf16[192,1536]{1,0:T(8,128)(2,1)}, u32[]{:S(2)}, u32[]{:S(2)}) collective-permute-start(bf16[192,1536]{1,0:T(8,128)(2,1)} %collective-permute-done.2.fc01), channel_id=1, source_target_pairs={{0,2},{2,0},{4,6},{6,4},{8,10},{10,8},{12,14},{14,12},{16,18},{18,... | collective-permute-start | bytes 1769480 | tf_op jit(solution)/shard_map/ppermute | solution.py:218
  136.1 5.4 %collective-permute-start.11 = (bf16[192,1536]{1,0:T(8,128)(2,1)}, bf16[192,1536]{1,0:T(8,128)(2,1)}, u32[]{:S(2)}, u32[]{:S(2)}) collective-permute-start(bf16[192,1536]{1,0:T(8,128)(2,1)} %collective-permute-done.fc10), channel_id=1, source_target_pairs={{0,2},{2,0},{4,6},{6,4},{8,10},{10,8},{12,14},{14,12},{16,18},{18,... | collective-permute-start | bytes 1769480 | tf_op jit(solution)/shard_map/ppermute | solution.py:218
  136.3 9.1 %collective-permute-start.13 = (bf16[384,1536]{1,0:T(8,128)(2,1)}, bf16[384,1536]{1,0:T(8,128)(2,1)S(1)}, u32[]{:S(2)}, u32[]{:S(2)}) collective-permute-start(bf16[384,1536]{1,0:T(8,128)(2,1)} %pad_maximum_fusion.pr00), channel_id=1, source_target_pairs={{0,2},{2,0},{4,6},{6,4},{8,10},{10,8},{12,14},{14,12},{16,18},{18,... | collective-permute-start | bytes 3538952 | tf_op jit(solution)/shard_map/ppermute | solution.py:218
  136.6 8.8 %collective-permute-start.14 = (bf16[384,1536]{1,0:T(8,128)(2,1)}, bf16[384,1536]{1,0:T(8,128)(2,1)}, u32[]{:S(2)}, u32[]{:S(2)}) collective-permute-start(bf16[384,1536]{1,0:T(8,128)(2,1)} %collective-permute-done.4.pr10), channel_id=1, source_target_pairs={{0,2},{2,0},{4,6},{6,4},{8,10},{10,8},{12,14},{14,12},{16,18},{18,... | collective-permute-start | bytes 3538952 | tf_op jit(solution)/shard_map/ppermute | solution.py:218
  136.8 8.6 %collective-permute-start.7 = (bf16[1024,384]{1,0:T(8,128)(2,1)S(1)}, bf16[1024,384]{1,0:T(8,128)(2,1)S(1)}, u32[]{:S(2)}, u32[]{:S(2)}) collective-permute-start(bf16[1024,384]{1,0:T(8,128)(2,1)S(1)} %get-tuple-element.126.orr), channel_id=1, source_target_pairs={{0,2},{2,0},{4,6},{6,4},{8,10},{10,8},{12,14},{14,12},{16,18},{18,... | collective-permute-start | bytes 2359304 | tf_op jit(solution)/shard_map/ppermute | solution.py:218
  141.5 3.0 collective-permute-start.12
  141.5 3.9 %collective-permute-start.9 = (bf16[192,1536]{1,0:T(8,128)(2,1)}, bf16[192,1536]{1,0:T(8,128)(2,1)}, u32[]{:S(2)}, u32[]{:S(2)}) collective-permute-start(bf16[192,1536]{1,0:T(8,128)(2,1)} %bitcast.13.fc00), channel_id=1, source_target_pairs={{0,2},{2,0},{4,6},{6,4},{8,10},{10,8},{12,14},{14,12},{16,18},{18,... | collective-permute-start | bytes 1769480 | tf_op jit(solution)/shard_map/ppermute | solution.py:218
  201.4 4.8 %collective-permute-start.17 = (bf16[2,384,1536]{2,1,0:T(8,128)(2,1)}, bf16[2,384,1536]{2,1,0:T(8,128)(2,1)S(1)}, u32[]{:S(2)}, u32[]{:S(2)}) collective-permute-start(bf16[2,384,1536]{2,1,0:T(8,128)(2,1)} %get-tuple-element.120), channel_id=1, source_target_pairs={{0,2},{2,0},{4,6},{6,4},{8,10},{10,8},{12,14},{14,12},{16,18},{18,... | collective-permute-start | bytes 7077896 | tf_op jit(solution)/shard_map/ppermute | solution.py:218
  201.9 7.8 %collective-permute-start.15 = (bf16[2,384,1536]{2,1,0:T(8,128)(2,1)}, bf16[2,384,1536]{2,1,0:T(8,128)(2,1)S(1)}, u32[]{:S(2)}, u32[]{:S(2)}) collective-permute-start(bf16[2,384,1536]{2,1,0:T(8,128)(2,1)} %get-tuple-element.116), channel_id=1, source_target_pairs={{0,2},{2,0},{4,6},{6,4},{8,10},{10,8},{12,14},{14,12},{16,18},{18,... | collective-permute-start | bytes 7077896 | tf_op jit(solution)/shard_map/ppermute | solution.py:218
  202.0 9.6 %collective-permute-start.16 = (bf16[1024,384]{1,0:T(8,128)(2,1)}, bf16[1024,384]{1,0:T(8,128)(2,1)S(1)}, u32[]{:S(2)}, u32[]{:S(2)}) collective-permute-start(bf16[1024,384]{1,0:T(8,128)(2,1)} %get-tuple-element.118), channel_id=1, source_target_pairs={{0,2},{2,0},{4,6},{6,4},{8,10},{10,8},{12,14},{14,12},{16,18},{18,... | collective-permute-start | bytes 2359304 | tf_op jit(solution)/shard_map/ppermute | solution.py:218
  206.2 41.4 %copy-start.14 = (bf16[2,384,1536]{2,1,0:T(8,128)(2,1)}, bf16[2,384,1536]{2,1,0:T(8,128)(2,1)S(1)}, u32[]{:S(2)}) copy-start(bf16[2,384,1536]{2,1,0:T(8,128)(2,1)S(1)} %collective-permute-done.17) | copy-start | bytes 7077892
  211.6 36.0 %collective-permute-start.18 = (bf16[384,1536]{1,0:T(8,128)(2,1)}, bf16[384,1536]{1,0:T(8,128)(2,1)S(1)}, u32[]{:S(2)}, u32[]{:S(2)}) collective-permute-start(bf16[384,1536]{1,0:T(8,128)(2,1)} %fusion), channel_id=1, source_target_pairs={{0,1},{1,0},{2,3},{3,2},{4,5},{5,4},{6,7},{7,6},{8,9},{9,8},{10,11... | collective-permute-start | bytes 3538952 | tf_op jit(solution)/shard_map/ppermute | solution.py:219
  213.6 34.0 %collective-permute-start.19 = (bf16[2,192,1536]{2,1,0:T(8,128)(2,1)}, bf16[2,192,1536]{2,1,0:T(8,128)(2,1)}, u32[]{:S(2)}, u32[]{:S(2)}) collective-permute-start(bf16[2,192,1536]{2,1,0:T(8,128)(2,1)} %add_convert_fusion), channel_id=1, source_target_pairs={{0,4},{2,6},{4,0},{6,2},{8,12},{10,14},{12,8},{14,10},{16,20},{18,... | collective-permute-start | bytes 3538952 | tf_op jit(solution)/shard_map/ppermute | solution.py:218
  247.6 35.8 %collective-permute-start.22 = (bf16[1024,1152]{1,0:T(8,128)(2,1)}, bf16[1024,1152]{1,0:T(8,128)(2,1)}, u32[]{:S(2)}, u32[]{:S(2)}) collective-permute-start(bf16[1024,1152]{1,0:T(8,128)(2,1)} %get-tuple-element.144), channel_id=1, source_target_pairs={{0,2},{2,0},{4,6},{6,4},{8,10},{10,8},{12,14},{14,12},{16,18},{18,... | collective-permute-start | bytes 7077896 | tf_op jit(solution)/shard_map/ppermute | solution.py:218
  252.3 16.1 %collective-permute-start.20 = (bf16[192,1536]{1,0:T(8,128)(2,1)}, bf16[192,1536]{1,0:T(8,128)(2,1)}, u32[]{:S(2)}, u32[]{:S(2)}) collective-permute-start(bf16[192,1536]{1,0:T(8,128)(2,1)} %fusion.2), channel_id=1, source_target_pairs={{0,4},{2,6},{4,0},{6,2},{8,12},{10,14},{12,8},{14,10},{16,20},{18,... | collective-permute-start | bytes 1769480 | tf_op jit(solution)/shard_map/ppermute | solution.py:218
  253.4 15.7 %collective-permute-start.21 = (bf16[192,1536]{1,0:T(8,128)(2,1)}, bf16[192,1536]{1,0:T(8,128)(2,1)S(1)}, u32[]{:S(2)}, u32[]{:S(2)}) collective-permute-start(bf16[192,1536]{1,0:T(8,128)(2,1)} %fusion.6), channel_id=1, source_target_pairs={{0,1},{1,0},{2,3},{3,2},{4,5},{5,4},{6,7},{7,6},{8,9},{9,8},{10,11... | collective-permute-start | bytes 1769480 | tf_op jit(solution)/shard_map/ppermute | solution.py:219
  272.4 106.5 %collective-permute-start.29 = (bf16[1024,768]{1,0:T(8,128)(2,1)}, bf16[1024,768]{1,0:T(8,128)(2,1)S(1)}, u32[]{:S(2)}, u32[]{:S(2)}) collective-permute-start(bf16[1024,768]{1,0:T(8,128)(2,1)} %get-tuple-element.143), channel_id=1, source_target_pairs={{1,2},{2,1},{5,6},{6,5},{9,10},{10,9},{13,14},{14,13},{17,18},{18,... | collective-permute-start | bytes 4718600 | tf_op jit(solution)/shard_map/ppermute | solution.py:1009
  274.0 94.3 %collective-permute-start.23 = (bf16[48,1536]{1,0:T(8,128)(2,1)}, bf16[48,1536]{1,0:T(8,128)(2,1)S(1)}, u32[]{:S(2)}, u32[]{:S(2)}) collective-permute-start(bf16[48,1536]{1,0:T(8,128)(2,1)} %get-tuple-element.253), channel_id=1, source_target_pairs={{0,16},{2,18},{4,20},{6,22},{8,24},{10,26},{12,28},{14,30},{16,0},... | collective-permute-start | bytes 442376 | tf_op jit(solution)/shard_map/ppermute | solution.py:564
  281.0 90.2 %collective-permute-start.24 = (bf16[48,1536]{1,0:T(8,128)(2,1)}, bf16[48,1536]{1,0:T(8,128)(2,1)}, u32[]{:S(2)}, u32[]{:S(2)}) collective-permute-start(bf16[48,1536]{1,0:T(8,128)(2,1)} %get-tuple-element.252), channel_id=1, source_target_pairs={{0,8},{2,10},{4,12},{6,14},{8,0},{10,2},{12,4},{14,6},{16,24},{18,... | collective-permute-start | bytes 442376 | tf_op jit(solution)/shard_map/ppermute | solution.py:564
  281.0 91.1 %collective-permute-start.25 = (bf16[48,1536]{1,0:T(8,128)(2,1)}, bf16[48,1536]{1,0:T(8,128)(2,1)}, u32[]{:S(2)}, u32[]{:S(2)}) collective-permute-start(bf16[48,1536]{1,0:T(8,128)(2,1)} %get-tuple-element.251), channel_id=1, source_target_pairs={{0,24},{2,26},{4,28},{6,30},{8,16},{10,18},{12,20},{14,22},{16,8},... | collective-permute-start | bytes 442376 | tf_op jit(solution)/shard_map/ppermute | solution.py:564
  283.3 88.8 %collective-permute-start.26 = (bf16[48,1536]{1,0:T(8,128)(2,1)}, bf16[48,1536]{1,0:T(8,128)(2,1)}, u32[]{:S(2)}, u32[]{:S(2)}) collective-permute-start(bf16[48,1536]{1,0:T(8,128)(2,1)} %get-tuple-element.250), channel_id=1, source_target_pairs={{0,16},{2,18},{4,20},{6,22},{8,24},{10,26},{12,28},{14,30},{16,0},... | collective-permute-start | bytes 442376 | tf_op jit(solution)/shard_map/ppermute | solution.py:564
  368.3 7.5 %collective-permute-start.27 = (bf16[48,1536]{1,0:T(8,128)(2,1)}, bf16[48,1536]{1,0:T(8,128)(2,1)S(1)}, u32[]{:S(2)}, u32[]{:S(2)}) collective-permute-start(bf16[48,1536]{1,0:T(8,128)(2,1)} %get-tuple-element.249), channel_id=1, source_target_pairs={{0,8},{2,10},{4,12},{6,14},{8,0},{10,2},{12,4},{14,6},{16,24},{18,... | collective-permute-start | bytes 442376 | tf_op jit(solution)/shard_map/ppermute | solution.py:564
  371.2 7.7 %collective-permute-start.28 = (bf16[48,1536]{1,0:T(8,128)(2,1)}, bf16[48,1536]{1,0:T(8,128)(2,1)S(1)}, u32[]{:S(2)}, u32[]{:S(2)}) collective-permute-start(bf16[48,1536]{1,0:T(8,128)(2,1)} %get-tuple-element.248), channel_id=1, source_target_pairs={{0,24},{2,26},{4,28},{6,30},{8,16},{10,18},{12,20},{14,22},{16,8},... | collective-permute-start | bytes 442376 | tf_op jit(solution)/shard_map/ppermute | solution.py:564
  (22 other events, 151.7 us)
where the time goes:
time: 396 us; the launch traced here: 388 us
  Pallas kernels  269 us (68%)
  starting transfers between devices  32.2 us (8%)
  waiting for transfers between devices  29.6 us (7%)
  local copies, waits for them, and re-layouts  29.5 us (7%)
  other arithmetic  22.6 us (6%)
  matrix products  3.99 us (1%)
    pallas_call x1, Pallas kernels, head(): pl.pallas_call(functools.partial(head_kernel, groups, chunks), in_specs=[...  57.9 us
    pallas_call x1, Pallas kernels, tail(): pl.pallas_call(functools.partial(tail_kernel, groups), in_specs=[VM] * 7,...  55.5 us
    pallas_call x1, Pallas kernels, feed_part(): pl.pallas_call(functools.partial(feed_kernel, rows), grid_spec=pltpu.Pref...  54.7 us
    pallas_call x4, Pallas kernels, one_call(): pl.pallas_call(kernel, grid_spec=pltpu.PrefetchScalarGridSpec(num_scalar_...  45.8 us
    pallas_call x1, Pallas kernels, attn_bwd(): pl.pallas_call(bwd_kernel, in_specs=[SM] + [VM] * 8, out_specs=[VM] * 2,...  33.1 us
    pallas_call x1, Pallas kernels, attn_fwd(): pl.pallas_call(fwd_kernel, in_specs=[SM, VM, VM, VM], out_specs=[VM] * 3,...  21.5 us
    ppermute x4, waiting for transfers between devices, exchange(): return lax.ppermute(value, 'tensor', [(0, 1), (1, 0)])  15.7 us
    ppermute x6, starting transfers between devices, far_exchange(): lax.ppermute(piece, 'dp', [(i, i ^ mask) for i in range(dp_size)])  13.8 us
  transfers between devices with their start and end apart: 30, of which 8 were waited for; matrix products, arithmetic and copies ran while one was open for 7% of the time, Pallas kernels for 37%

commit v1 on v0

--- a/solution.py
+++ b/solution.py
@@ -38,12 +38,16 @@
     mid=jnp.clip((blocks[:,QB-1]+QB-1)//QB,low,idx)
     return starts.reshape(1,n), jnp.concatenate([jnp.reshape(core,(1,)),low,mid]).astype(jnp.int32)
 
-def attn_masks(kat, srow, diagonal):
+def attn_mask(kat, at, srow):
     keys = lax.broadcasted_iota(jnp.int32, (QB, QB), 0)
-    mask = keys >= (srow - kat)
-    if diagonal:
-        mask = mask & (keys <= lax.broadcasted_iota(jnp.int32, (QB, QB), 1))
-    return mask
+    rows = lax.broadcasted_iota(jnp.int32, (1, QB), 1) + (at - kat)
+    return (keys >= srow - kat) & (keys <= rows)
+
+
+def over_blocks(info, i, nb, step, carry):
+    low, mid = info[1 + i], info[1 + nb + i]
+    carry = lax.fori_loop(0, mid - low + 1, lambda k, c: step(True, jnp.where(k == 0, i, low + k - 1), c), carry)
+    return lax.fori_loop(mid, i, functools.partial(step, False), carry)
 
 
 def head_lanes(values):
@@ -71,16 +75,16 @@
         srow = st_ref[:, qr]
         acc[...] = jnp.zeros_like(acc)
 
-        def step(mode, j, carry):
+        def step(masked, j, carry):
             kat = pl.multiple_of(j * QB, QB)
             kr = pl.ds(kat, QB)
-            if mode:
-                mask = attn_masks(kat, srow, mode == 2)
+            if masked:
+                mask = attn_mask(kat, at, srow)
             scores, mixed = [], []
             for h in range(heads):
                 lanes = slice(h // 2 * 128, h // 2 * 128 + 128)
                 one = lax.dot_general(ks[kr, lanes], qm[h % 2, qr, lanes], NT, preferred_element_type=f32)
-                scores.append(jnp.where(mask, one, NEG) if mode else one)
+                scores.append(jnp.where(mask, one, NEG) if masked else one)
             for h in range(heads):
                 top, total = carry[h]
                 new = jnp.maximum(top, jnp.max(scores[h], axis=0, keepdims=True))
@@ -93,9 +97,7 @@
                 acc[sub] = mixed[h][2] * acc[sub] + jnp.dot(vt[sub, kr], mixed[h][3], preferred_element_type=f32)
             return tuple(m[:2] for m in mixed)
 
-        carry = step(2, i, ((jnp.full((1, QB), NEG, f32), jnp.zeros((1, QB), f32)),) * heads)
-        carry = lax.fori_loop(info[1 + i], info[1 + nb + i], functools.partial(step, 1), carry)
-        carry = lax.fori_loop(info[1 + nb + i], i, functools.partial(step, 0), carry)
+        carry = over_blocks(info, i, nb, step, ((jnp.full((1, QB), NEG, f32), jnp.zeros((1, QB), f32)),) * heads)
         for h, (top, total) in enumerate(carry):
             sub = slice(h * HD, (h + 1) * HD)
             acc[sub] = acc[sub] / total
@@ -152,17 +154,17 @@
         srow = st_ref[:, qr]
         dqs[...] = jnp.zeros_like(dqs)
 
-        def step(mode, j, carry):
+        def step(masked, j, carry):
             kat = pl.multiple_of(j * QB, QB)
             kr = pl.ds(kat, QB)
-            if mode:
-                mask = attn_masks(kat, srow, mode == 2)
+            if masked:
+                mask = attn_mask(kat, at, srow)
             scores, softs, grads = [], [], []
             for h in range(heads):
                 lanes = lanes_of(h // 2)
                 one = lax.dot_general(ks[kr, lanes], qm[h % 2, qr, lanes], NT, preferred_element_type=f32)
                 back = lax.dot_general(vs[kr, lanes], dom[h % 2, qr, lanes], NT, preferred_element_type=f32)
-                scores.append((jnp.where(mask, one, NEG) if mode else one, back))
+                scores.append((jnp.where(mask, one, NEG) if masked else one, back))
             for h in range(heads):
                 soft = jnp.exp(scores[h][0] - lse_ref[h : h + 1, qr])
                 grads.append((soft * (scores[h][1] - dlt[h : h + 1, qr])).astype(bf))
@@ -178,9 +180,7 @@
                     dqs[sub] += jnp.dot(kt[sub, kr], grads[h], preferred_element_type=f32)
             return carry
 
-        step(2, i, 0)
-        lax.fori_loop(info[1 + i], info[1 + nb + i], functools.partial(step, 1), 0)
-        lax.fori_loop(info[1 + nb + i], i, functools.partial(step, 0), 0)
+        over_blocks(info, i, nb, step, 0)
         qm[0, qr] = (dqs[...] * (HD**-0.5)).T.astype(bf)
         return 0
 
@@ -238,7 +238,7 @@
     cuts = [128 * ((tiles * k) // count) for k in range(count + 1)]
     arrays = range(which, until + 1) if until else (which,)
     return tuple(
-        (array, low, high - low, 128 * max(1, (high - low) * 2 // 3 // 128))
+        (array, low, high - low, high - low - 128)
         for low, high in zip(cuts, cuts[1:]) for array in arrays)
 
 
@@ -393,8 +393,8 @@
     )(tokens, *shards)
 
 
-def tail_kernel(groups, tokens, own_lo, own_hi, rest_lo, rest_hi, small_lo, small_hi, x_out, total, vecs,
-                part, got_core, got_near, got_last, got_far, vec, vec_core, vec_two, vec_one, vec_far, send_sem, recv_sem, local_sem):
+def tail_kernel(groups, tokens, own_lo, own_hi, rest_lo, rest_hi, small_lo, small_hi, feed, x_out, total, vecs, feed_total,
+                feed_part, feed_got, part, got_core, got_near, got_last, got_far, vec, vec_core, vec_two, vec_one, vec_far, send_sem, recv_sem, local_sem):
     dp, t = lax.axis_index("dp"), lax.axis_index("tensor")
     core = dp % 2
     away = core + t - 2 * core * t
@@ -438,6 +438,19 @@
     @pl.when(away == 0)
     def _():
         stay_copy.start()
+
+    feed_steps = []
+    held, used = feed.shape[0], 0
+    for number, group in enumerate(reversed(groups)):
+        moves = group_moves(group)
+        held //= len(moves) + 1
+        source, step = feed if number == 0 else feed_part, []
+        for place, bits in moves:
+            step.append(remote(source.at[pl.ds(place * held, held)], feed_got.at[pl.ds(used, held)], (flip(dp, bits), t)))
+            used += held
+        feed_steps.append((step, source, held, used - held * len(moves), len(moves)))
+    for move in feed_steps[0][0]:
+        move.start()
 
     def add(*terms):
         out = terms[0].astype(f32)
@@ -515,6 +528,25 @@
 
         lax.fori_loop(0, held, sum_far, 0)
         to_far += step
+    for number, (step, source, held, base, moves) in enumerate(feed_steps):
+        if number > 0:
+            for move in step:
+                move.start()
+        for move in step:
+            move.wait_recv()
+
+        def sum_feed(k, _, source=source, held=held, base=base, moves=moves):
+            feed_part[k] = add(source[k], *[feed_got[base + m * held + k] for m in range(moves)])
+            return 0
+
+        if number + 1 < len(feed_steps):
+            lax.fori_loop(0, held, sum_feed, 0)
+        else:
+            out = source[0].astype(f32)
+            for m in range(moves):
+                out = out + feed_got[base + m * held].astype(f32)
+            feed_total[...] = out
+        to_far += step
     total[...] = part[mine, 0].astype(f32)
     vecs[...] = vec_one[0].astype(f32)
 
@@ -530,56 +562,29 @@
         move.wait_send()
 
 
-def tail(dp_size, tokens, own, rest, small):
+def tail(dp_size, tokens, own, rest, small, feed):
     groups = far_groups(dp_size)
     half, rows, cols = own[0].shape
     quarter = half // 2
     wide = small[0].shape[2]
     partners = sum(len(group_moves(g)) for g in groups)
-    slots = 11 + 2 * partners
+    slots = 11 + 3 * partners
     return pl.pallas_call(
         functools.partial(tail_kernel, groups),
-        in_specs=[VM] * 7,
-        out_specs=[ANY, VM, VM],
+        in_specs=[VM] * 8,
+        out_specs=[ANY, VM, VM, VM],
         out_shape=[
             jax.ShapeDtypeStruct(tokens.shape, bf), jax.ShapeDtypeStruct((rows, cols), f32),
-            jax.ShapeDtypeStruct((rows, wide), f32)],
+            jax.ShapeDtypeStruct((rows, wide), f32), jax.ShapeDtypeStruct(feed.shape[1:], f32)],
         scratch_shapes=[
+            pltpu.VMEM(feed.shape, bf), pltpu.VMEM(feed.shape, bf),
             pltpu.VMEM((2, half, rows, cols), bf), pltpu.VMEM((2, half, rows, cols), bf), pltpu.VMEM((2, half, rows, cols), bf),
             pltpu.VMEM((quarter, rows, cols), bf), pltpu.VMEM((quarter, rows, cols), bf),
             pltpu.VMEM((half, rows, wide), bf), pltpu.VMEM((half, rows, wide), bf), pltpu.VMEM((quarter, rows, wide), bf),
             pltpu.VMEM((quarter, rows, wide), bf), pltpu.VMEM((quarter, rows, wide), bf),
             pltpu.SemaphoreType.DMA((slots,)), pltpu.SemaphoreType.DMA((slots,)), pltpu.SemaphoreType.DMA((1,))],
         compiler_params=pltpu.CompilerParams(collective_id=1, has_side_effects=True, vmem_limit_bytes=48 << 20),
-    )(tokens, *own, *rest, *small)
-
-
-def far_exchange(value, dp_size):
-    out, held = [], value.shape[0]
-    (group,) = far_groups(dp_size)[-1:]
-    held //= len(group_moves(group)) + 1
-    for place, bits in group_moves(group):
-        mask = sum(bits)
-        piece = value[place * held : (place + 1) * held]
-        out.append(lax.ppermute(piece, "dp", [(i, i ^ mask) for i in range(dp_size)]))
-    return out
-
-
-def far_sum(value, got, dp_size):
-    held = got[0].shape[0]
-    total = value[:held].astype(f32)
-    for piece in got:
-        total = total + piece.astype(f32)
-    for group in far_groups(dp_size)[-2::-1]:
-        total = total.astype(bf)
-        held //= len(group_moves(group)) + 1
-        moves = [
-            lax.ppermute(total[place * held : (place + 1) * held], "dp", [(i, i ^ sum(bits)) for i in range(dp_size)])
-            for place, bits in group_moves(group)]
-        total = total[:held].astype(f32)
-        for piece in moves:
-            total = total + piece.astype(f32)
-    return total
+    )(tokens, *own, *rest, *small, feed)
 
 
 def add_low(*terms):
@@ -636,30 +641,25 @@
 
 def first_kernel(rows, info, tokens, pack, weight, x_out, n1_out, send, vec_rel, vec_nat, order):
     width, cols = tokens.shape[1], weight.shape[2] // 3
-    order[...] = order_matrix(info[1], rows, width)
-    small = pack[0, :, cols:].astype(f32).T[:VECS]
-    vec_rel[...] = small
-    vec_nat[...] = lax.dot_general(small.astype(bf), order[...], NT, preferred_element_type=f32)
-    bias = bias_row(vec_nat, 1 - info[0], cols)
-
-    def body(at):
-        x = jnp.dot(tokens[at], order[...], preferred_element_type=f32)
-        hat, _ = norm_parts(x)
-        n1 = (hat * vec_rel[0:1] + vec_rel[1:2]).astype(bf)
-        x_out[at] = x.astype(bf)
-        n1_out[at] = n1
-        send[at] = (jnp.dot(n1, weight[0], preferred_element_type=f32) + bias).astype(bf)
-
-    over_rows(tokens.shape[0], body)
+
+    @pl.when(pl.program_id(0) == 0)
+    def _():
+        order[...] = order_matrix(info[1], rows, width)
+        small = pack[0, :, cols:].astype(f32).T[:VECS]
+        vec_rel[...] = small
+        vec_nat[...] = lax.dot_general(small.astype(bf), order[...], NT, preferred_element_type=f32)
+
+    x = jnp.dot(tokens[...], order[...], preferred_element_type=f32)
+    hat, _ = norm_parts(x)
+    n1 = (hat * vec_rel[0:1] + vec_rel[1:2]).astype(bf)
+    x_out[...] = x.astype(bf)
+    n1_out[...] = n1
+    send[...] = (jnp.dot(n1, weight[0], preferred_element_type=f32) + bias_row(vec_nat, 1 - info[0], cols)).astype(bf)
 
 
 def own_kernel(info, n1, weight, vec_nat, out):
     bias = bias_row(vec_nat, info[0], weight.shape[2] // 3)
-
-    def body(at):
-        out[at] = (jnp.dot(n1[at], weight[0], preferred_element_type=f32) + bias).astype(bf)
-
-    over_rows(n1.shape[0], body)
+    out[...] = (jnp.dot(n1[...], weight[0], preferred_element_type=f32) + bias).astype(bf)
 
 
 def picked(array, index):
@@ -686,16 +686,37 @@
     return jax.ShapeDtypeStruct(shape, dtype)
 
 
+def by_rows(kernel, info, inputs, specs, outs, scratch=(), flops=1 << 22):
+    total = inputs[0].shape[0]
+
+    def spec(array, given=None):
+        if given is not None:
+            return given
+        if array.shape[0] == total:
+            return pl.BlockSpec((ROWS,) + array.shape[1:], lambda k, s: (k, 0))
+        return whole(array)
+
+    return pl.pallas_call(
+        kernel,
+        grid_spec=pltpu.PrefetchScalarGridSpec(
+            num_scalar_prefetch=1, grid=(total // ROWS,), in_specs=[spec(a, g) for a, g in zip(inputs, specs)],
+            out_specs=[spec(o) for o in outs], scratch_shapes=list(scratch)),
+        out_shape=outs,
+        cost_estimate=pl.CostEstimate(flops=flops, bytes_accessed=1 << 18, transcendentals=0),
+        compiler_params=pltpu.CompilerParams(vmem_limit_bytes=24 << 20),
+    )(info, *inputs)
+
+
 def project_first(info, rows, tokens, packs, weights):
     n, width = tokens.shape
-    return one_call(
+    return by_rows(
         functools.partial(first_kernel, rows), info, (tokens, packs, weights), (None, picked(packs, 0), picked(weights, 1)),
         [like((n, width), bf), like((n, width), bf), like((n, weights.shape[2]), bf), like((VECS, width), f32), like((VECS, width), f32)],
-        [pltpu.VMEM((width, width), bf)])
+        [pltpu.VMEM((width, width), bf)], 1 << 36)
 
 
 def project_own(info, n1, weights, vec_nat):
-    (out,) = one_call(
+    (out,) = by_rows(
         own_kernel, info, (n1, weights, vec_nat), (None, picked(weights, 0), None), [like((n1.shape[0], weights.shape[2]), bf)])
     return out
 
@@ -965,11 +986,11 @@
     part = jnp.stack([core, dp_pos, jnp.where(mine, 1, 0)]).astype(jnp.int32)
     x, n1, qkv_send, vec_rel, vec_nat = project_first(part, rows, tokens, all_out, all_qkv)
     qkv_recv = exchange(qkv_send, 1, dp_size)
-    fc_parts, proj_half, n1 = lax.optimization_barrier((fc_parts, proj_half, n1))
+    qkv_own = project_own(part, n1, all_qkv, vec_nat)
+    fc_parts, proj_half, qkv_own = lax.optimization_barrier((fc_parts, proj_half, qkv_own))
     fc_parts = [p + [exchange(p[0], 2, dp_size)] for p in fc_parts]
     proj_half = jnp.concatenate([proj_far, proj_half], axis=0)
     proj_parts = [[proj_half], [exchange(proj_half, 0, dp_size)]]
-    qkv_own = project_own(part, n1, all_qkv, vec_nat)
     starts, info = attn_info(seg, core)
     o_own, o_send, lse = attn_fwd(qkv_own, qkv_recv, starts, info)
     fc_parts, proj_parts, o_own, o_send = lax.optimization_barrier((fc_parts, proj_parts, o_own, o_send))
@@ -993,9 +1014,10 @@
     last, fc_rest, pr_rest = lax.optimization_barrier((last, fc_rest, pr_rest))
     fc_sent = exchange(fc_rest, 0, dp_size)
     pr_sent = exchange(pr_rest, 2, dp_size)
+    block_recv = lax.ppermute(block_out, BOTH, swap)
     dq_own, dq_send = attn_bwd(*last, starts, lse, info)
     dq_recv = exchange(dq_send, 1, dp_size)
-    dq_own, fc_sent, pr_sent, block_out = lax.optimization_barrier((dq_own, fc_sent, pr_sent, block_out))
+    dq_own, fc_sent, pr_sent = lax.optimization_barrier((dq_own, fc_sent, pr_sent))
     fc_rest = add_low(fc_lo[0, near_size:], fc_got[0, near_size:], fc_sent[near_size:])
     pr_rest = add_low(pr_lo[1, :near_size], pr_got[1, :near_size], pr_sent[1])
     dq_own, fc_rest, pr_rest = lax.optimization_barrier((dq_own, fc_rest, pr_rest))
@@ -1005,22 +1027,18 @@
     d_n1, fc_near, pr_near = lax.optimization_barrier((d_n1, fc_near, pr_near))
     sum_fc = add_low(fc_lo[0, :near_size], fc_got[0, :near_size], fc_sent[:near_size], fc_near)
     sum_proj = add_low(pr_lo[0, :near_size], pr_got[0, :near_size], pr_sent[0], pr_near)
-    d_n1, sum_fc, sum_proj, block_out = lax.optimization_barrier((d_n1, sum_fc, sum_proj, block_out))
-    block_recv = lax.ppermute(block_out, BOTH, swap)
-    fc_sent = far_exchange(sum_fc, dp_size)
-    proj_sent = far_exchange(sum_proj, dp_size)
-    own_lo, own_hi, d_n1, own_sums = last_own(part, dq_own, n1, d_attn, o_own, all_qkv)
+    feed = jnp.concatenate([sum_fc, sum_proj], axis=1).reshape(-1, rows, 2 * hidden)
+    d_n1, feed = lax.optimization_barrier((d_n1, feed))
     rest_lo, rest_hi, grad_tokens, d_small = last_part(
         part, rows, dq_recv, n1, d_attn, o_recv, all_qkv, d_n1, x, d_middle, vec_rel, own_sums, mid_sums, fc_rows)
     blocks = lambda arr: arr.reshape(dp_size // 2, rows, -1)
-    grad_tokens, sum_a, vecs = tail(
+    grad_tokens, sum_a, vecs, sum_feed = tail(
         dp_size, grad_tokens, (blocks(own_lo), blocks(own_hi)), (blocks(rest_lo), blocks(rest_hi)),
-        (blocks(d_small[:half]), blocks(d_small[half:])))
-    vecs, fc_sent, proj_sent, block_recv = lax.optimization_barrier((vecs, fc_sent, proj_sent, block_recv))
+        (blocks(d_small[:half]), blocks(d_small[half:])), feed)
+    vecs, block_recv = lax.optimization_barrier((vecs, block_recv))
     block_out = jnp.where(mine, block_out, block_recv)
     owner = dp_pos - core + t_pos
     grad_tokens = dot(grad_tokens, order_matrix(owner, rows, width), NT).astype(bf)
-    sum_fc, sum_proj = far_sum(sum_fc, fc_sent, dp_size), far_sum(sum_proj, proj_sent, dp_size)
     return (
         block_out,
         grad_tokens,
@@ -1032,9 +1050,9 @@
         vecs[:, 4],
         vecs[:, 5],
         vecs[:, 6],
-        sum_fc.astype(f32),
+        sum_feed[:, :hidden],
         vecs[:, 8 : 8 + fan].reshape(rows * fan),
-        sum_proj.astype(f32).T,
+        sum_feed[:, hidden:].T,
         vecs[:, 7],
     )
 

time: 396 us -> 369 us (0.932)
  waiting for transfers between devices: 29.6 us -> 16.5 us
  starting transfers between devices: 32.2 us -> 27.4 us
    pallas_call x4 -> x2, Pallas kernels: 45.8 us -> 27.7 us  [one_call(): pl.pallas_call(kernel, grid_spec=pltpu.PrefetchScalarGridSpec(num_scalar_...]
    pallas_call x1 -> x3, Pallas kernels: 55.5 us -> 70.1 us  [the longest x1 58.6 us: tail(): pl.pallas_call(functools.partial(tail_kernel, groups), in_specs=[VM] * 8,...]
    ppermute x6 -> x0, starting transfers between devices: 13.8 us -> none  [far_exchange(): lax.ppermute(piece, 'dp', [(i, i ^ mask) for i in range(dp_size)])]
    ppermute x18, starting transfers between devices: 12.3 us -> 20 us  [exchange(): return lax.ppermute(value, 'dp', [(i, i ^ bit) for i in range(dp_size)])]
    ppermute x6 -> x0, waiting for transfers between devices: 6.81 us -> none  [far_exchange(): lax.ppermute(piece, 'dp', [(i, i ^ mask) for i in range(dp_size)])]
    ppermute x4, waiting for transfers between devices: 15.7 us -> 8.96 us  [exchange(): return lax.ppermute(value, 'tensor', [(0, 1), (1, 0)])]
    unnamed x50 -> x66, local copies, waits for them, and re-layouts: 11 us -> 13.9 us
  transfers between devices with their start and end apart: 30 -> 24, of which waited for: 8 -> 5; matrix products, arithmetic and copies ran while one was open for 7% -> 5% of each run, Pallas kernels for 37% -> 40%
where the time goes in v1:
time: 369 us; the launch traced here: 362 us
  Pallas kernels  267 us (72%)
  local copies, waits for them, and re-layouts  28.4 us (8%)
  starting transfers between devices  27.4 us (7%)
  other arithmetic  19 us (5%)
  waiting for transfers between devices  16.5 us (4%)
    pallas_call x1, Pallas kernels, tail(): pl.pallas_call(functools.partial(tail_kernel, groups), in_specs=[VM] * 8,...  58.6 us
    pallas_call x1, Pallas kernels, head(): pl.pallas_call(functools.partial(head_kernel, groups, chunks), in_specs=[...  58.3 us
    pallas_call x1, Pallas kernels, feed_part(): pl.pallas_call(functools.partial(feed_kernel, rows), grid_spec=pltpu.Pref...  54.5 us
    pallas_call x1, Pallas kernels, attn_bwd(): pl.pallas_call(bwd_kernel, in_specs=[SM] + [VM] * 8, out_specs=[VM] * 2,...  33.5 us
    pallas_call x2, Pallas kernels, one_call(): pl.pallas_call(kernel, grid_spec=pltpu.PrefetchScalarGridSpec(num_scalar_...  27.7 us
    pallas_call x1, Pallas kernels, attn_fwd(): pl.pallas_call(fwd_kernel, in_specs=[SM, VM, VM, VM], out_specs=[VM] * 3,...  22.9 us
    ppermute x18, starting transfers between devices, exchange(): return lax.ppermute(value, 'dp', [(i, i ^ bit) for i in range(dp_size)])  20 us
    unnamed x66, local copies, waits for them, and re-layouts  13.9 us
  transfers between devices with their start and end apart: 24, of which 5 were waited for; matrix products, arithmetic and copies ran while one was open for 5% of the time, Pallas kernels for 40%

profile of v1, /device:TPU:0, one launch (start us, length us, event | category | flops | bytes accessed | tf_op | source)
XLA Modules:
  0.0 362.3 jit_solution(2880335612138732877)
XLA Ops:
  8.7 1.4 fusion.8.refs_1_
  10.1 58.3 %shard_map.254 = (bf16[1024,768]{1,0:T(8,128)(2,1)}, bf16[2,16,48,1152]{3,2,1,0:T(8,128)(2,1)}, bf16[2,16,48,512]{3,2,1,0:T(8,128)(2,1)}, bf16[4,48,1536]{2,1,0:T(8,128)(2,1)}, bf16[4,48,1536]{2,1,0:T(8,128)(2,1)}) custom-call(bf16[1024,768]{1,0:T(8,128)(2,1)} %tokens.1, bf16[48,1152]{1,0:T(8,128)(2,1)} %reshape.335.refs_0_, bf16[48,512]{1,0:T(8,128)(2,1)} %fusion.8.refs_1_, ...), custom_call_target="tpu_custom_call" | custom-call | tf_op jit(solution)/shard_map/pallas_call | solution.py:385
  68.4 2.0 copy-done
  70.4 1.4 copy-done.7
  71.8 1.4 copy-done.19
  73.3 8.2 %shard_map.255 = (bf16[1024,768]{1,0:T(8,128)(2,1)S(1)}, bf16[1024,768]{1,0:T(8,128)(2,1)S(1)}, bf16[1024,1152]{1,0:T(8,128)(2,1)}, f32[16,768]{1,0:T(8,128)S(1)}, f32[16,768]{1,0:T(8,128)S(1)}) custom-call(s32[3]{0:T(128)S(1)} %pad_add_fusion.info, bf16[1024,768]{1,0:T(8,128)(2,1)S(1)} %copy-done.19, bf16[2,768,512]{2,1,0:T(8,128)(2,1)S(1)} %bitcast.64, ...), custom_call_target="tpu_custom_call" | custom-call | flops 68719476736 | bytes 262144 | tf_op jit(solution)/shard_map/pallas_call | solution.py:699
  81.8 2.0 collective-permute-start.1
  83.8 3.3 shard_map.256.own
  87.2 1.4 copy-done.2
  88.6 8.9 %collective-permute-done.fc10 = bf16[192,1536]{1,0:T(8,128)(2,1)} collective-permute-done((bf16[192,1536]{1,0:T(8,128)(2,1)}, bf16[192,1536]{1,0:T(8,128)(2,1)}, u32[]{:S(2)}, u32[]{:S(2)}) %collective-permute-start) | collective-permute-done | bytes 589856 | tf_op jit(solution)/shard_map/ppermute | solution.py:219
  98.7 1.6 collective-permute-start.4
  100.3 1.8 collective-permute-start.8
  102.2 1.8 collective-permute-start.2
  104.8 22.9 %shard_map.257 = (bf16[1024,384]{1,0:T(8,128)(2,1)S(1)}, bf16[1024,384]{1,0:T(8,128)(2,1)S(1)}, f32[6,2048]{1,0:T(8,128)S(1)}) custom-call(s32[17]{0:T(128)S(1)} %pad_add_fusion.1.info, bf16[1024,1152]{1,0:T(8,128)(2,1)S(1)} %copy-done.3, bf16[1024,1152]{1,0:T(8,128)(2,1)} %collective-permute-done.6.recv, s32[1,2048]{1,0:T(1,128)S(1)} %bitcast.71), custom_call_target="tpu_custom_call" | custom-call | flops 4194304 | bytes 262144 | tf_op jit(solution)/shard_map/pallas_call | solution.py:116
  129.3 2.0 collective-permute-done.3.fc11
  132.3 11.0 %collective-permute-start.7 = (bf16[1024,384]{1,0:T(8,128)(2,1)S(1)}, bf16[1024,384]{1,0:T(8,128)(2,1)S(1)}, u32[]{:S(2)}, u32[]{:S(2)}) collective-permute-start(bf16[1024,384]{1,0:T(8,128)(2,1)S(1)} %get-tuple-element.121.orr), channel_id=1, source_target_pairs={{0,2},{2,0},{4,6},{6,4},{8,10},{10,8},{12,14},{14,12},{16,18},{18,... | collective-permute-start | bytes 2359304 | tf_op jit(solution)/shard_map/ppermute | solution.py:218
  148.5 54.5 %shard_map.258 = (bf16[1024,768]{1,0:T(8,128)(2,1)}, f32[1024,768]{1,0:T(8,128)}, bf16[1024,768]{1,0:T(8,128)(2,1)}, bf16[1024,384]{1,0:T(8,128)(2,1)}, bf16[102...) custom-call(s32[3]{0:T(128)} %copy-done.17, ...), custom_call_target="tpu_custom_call" | custom-call | flops 4194304 | bytes 262144 | tf_op jit(solution)/shard_map/pallas_call | solution.py:846
  204.0 3.9 %collective-permute-done.17 = bf16[2,384,1536]{2,1,0:T(8,128)(2,1)S(1)} collective-permute-done((bf16[2,384,1536]{2,1,0:T(8,128)(2,1)}, bf16[2,384,1536]{2,1,0:T(8,128)(2,1)S(1)}, u32[]{:S(2)}, u32[]{:S(2)}) %collective-permute-start.17) | collective-permute-done | bytes 2359328 | tf_op jit(solution)/shard_map/ppermute | solution.py:218
  207.9 3.5 add_convert_fusion
  211.4 1.6 fusion
  213.9 1.7 collective-permute-start.19
  215.6 1.5 collective-permute-start.20
  217.0 33.5 %shard_map.259 = (bf16[1024,1152]{1,0:T(8,128)(2,1)}, bf16[1024,1152]{1,0:T(8,128)(2,1)}) custom-call(s32[17]{0:T(128)} %copy-done.18, bf16[1024,1152]{1,0:T(8,128)(2,1)} %copy-done.2, bf16[1024,1152]{1,0:T(8,128)(2,1)} %collective-permute-done.6.recv, bf16[1024,384]{1,0:T(8,128)(2,1)} %get-tuple-element.118.doo, bf16[1024,384]{1,0:T(8,128)(2,1)} %copy-done.27, ...), custom_call_target="tpu_custom_call" | custom-call | flops 4194304 | bytes 262144 | tf_op jit(solution)/shard_map/pallas_call | solution.py:198
  250.5 2.7 fusion.6
  255.2 1.9 collective-permute-start.23
  258.4 12.1 %shard_map.260 = (bf16[384,1536]{1,0:T(8,128)(2,1)}, bf16[384,1536]{1,0:T(8,128)(2,1)}, f32[1024,768]{1,0:T(8,128)}, f32[8,1152]{1,0:T(8,128)}) custom-call(s32[3]{0:T(128)} %copy-done.17, bf16[1024,1152]{1,0:T(8,128)(2,1)} %get-tuple-element.131.d_qkv, bf16[1024,768]{1,0:T(8,128)(2,1)} %copy-done.4, bf16[1024,768]{1,0:T(8,128)(2,1)} %get-tuple-element.124.d_attn, ...), custom_call_target="tpu_custom_call" | custom-call | flops 4194304 | bytes 262144 | tf_op jit(solution)/shard_map/pallas_call | solution.py:674
  270.5 2.4 fusion.1
  274.1 15.6 %shard_map.261 = (bf16[384,1536]{1,0:T(8,128)(2,1)}, bf16[384,1536]{1,0:T(8,128)(2,1)}, bf16[1024,768]{1,0:T(8,128)(2,1)}, bf16[768,128]{1,0:T(8,128)(2,1)}) custom-call(s32[3]{0:T(128)} %copy-done.17, bf16[1024,1152]{1,0:T(8,128)(2,1)} %collective-permute-done.18.d_qkv, bf16[1024,768]{1,0:T(8,128)(2,1)} %copy-done.4, ...), custom_call_target="tpu_custom_call" | custom-call | flops 4194304 | bytes 262144 | tf_op jit(solution)/shard_map/pallas_call | solution.py:674
  291.9 1.3 copy-done.11
  293.2 58.6 %shard_map.262 = (bf16[1024,768]{1,0:T(8,128)(2,1)}, f32[48,1536]{1,0:T(8,128)S(1)}, f32[48,128]{1,0:T(8,128)S(1)}, f32[48,3072]{1,0:T(8,128)S(1)}) custom-call(bf16[1024,768]{1,0:T(8,128)(2,1)} %get-tuple-element.143.tokens, bf16[8,48,1536]{2,1,0:T(8,128)(2,1)S(1)} %bitcast.65, bf16[8,48,1536]{2,1,0:T(8,128)(2,1)S(1)} %bitcast.66, ...), custom_call_target="tpu_custom_call" | custom-call | tf_op jit(solution)/shard_map/pallas_call | solution.py:572
  353.4 2.7 broadcast_select_fusion
  359.3 2.6 convolution_convert_fusion
  (139 shorter events, 31.4 us)
Async XLA Ops:
  10.1 73.7 %copy-start.17 = (s32[3]{0:T(128)}, s32[3]{0:T(128)S(1)}, u32[]{:S(2)}) copy-start(s32[3]{0:T(128)S(1)} %pad_add_fusion.info) | copy-start | bytes 40
  81.4 23.4 %collective-permute-start.6 = (bf16[1024,1152]{1,0:T(8,128)(2,1)}, bf16[1024,1152]{1,0:T(8,128)(2,1)}, u32[]{:S(2)}, u32[]{:S(2)}) collective-permute-start(bf16[1024,1152]{1,0:T(8,128)(2,1)} %get-tuple-element.96), channel_id=1, source_target_pairs={{0,2},{2,0},{4,6},{6,4},{8,10},{10,8},{12,14},{14,12},{16,18},{18,... | collective-permute-start | bytes 7077896 | tf_op jit(solution)/shard_map/ppermute | solution.py:218
  81.8 15.8 %collective-permute-start = (bf16[192,1536]{1,0:T(8,128)(2,1)}, bf16[192,1536]{1,0:T(8,128)(2,1)}, u32[]{:S(2)}, u32[]{:S(2)}) collective-permute-start(bf16[192,1536]{1,0:T(8,128)(2,1)} %bitcast.13.fc00), channel_id=1, source_target_pairs={{0,1},{1,0},{2,3},{3,2},{4,5},{5,4},{6,7},{7,6},{8,9},{9,8},{10,11... | collective-permute-start | bytes 1769480 | tf_op jit(solution)/shard_map/ppermute | solution.py:219
  81.8 15.8 %collective-permute-start.1 = (bf16[192,1536]{1,0:T(8,128)(2,1)S(1)}, bf16[192,1536]{1,0:T(8,128)(2,1)S(1)}, u32[]{:S(2)}, u32[]{:S(2)}) collective-permute-start(bf16[192,1536]{1,0:T(8,128)(2,1)S(1)} %bitcast.76), channel_id=1, source_target_pairs={{0,4},{2,6},{4,0},{6,2},{8,12},{10,14},{12,8},{14,10},{16,20},{18,... | collective-permute-start | bytes 1769480 | tf_op jit(solution)/shard_map/ppermute | solution.py:218
  98.7 32.5 %collective-permute-start.4 = (bf16[384,1536]{1,0:T(8,128)(2,1)}, bf16[384,1536]{1,0:T(8,128)(2,1)}, u32[]{:S(2)}, u32[]{:S(2)}) collective-permute-start(bf16[384,1536]{1,0:T(8,128)(2,1)} %pad_maximum_fusion.pr00), channel_id=1, source_target_pairs={{0,1},{1,0},{2,3},{3,2},{4,5},{5,4},{6,7},{7,6},{8,9},{9,8},{10,11... | collective-permute-start | bytes 3538952 | tf_op jit(solution)/shard_map/ppermute | solution.py:219
  100.3 1.8 collective-permute-start.5
  100.3 31.9 %collective-permute-start.8 = (bf16[1024,768]{1,0:T(8,128)(2,1)}, bf16[1024,768]{1,0:T(8,128)(2,1)}, u32[]{:S(2)}, u32[]{:S(2)}) collective-permute-start(bf16[1024,768]{1,0:T(8,128)(2,1)} %cot.1), channel_id=1, source_target_pairs={{1,2},{2,1},{5,6},{6,5},{9,10},{10,9},{13,14},{14,13},{17,18},{18,... | collective-permute-start | bytes 4718600 | tf_op jit(solution)/shard_map/ppermute | solution.py:1000
  102.2 27.1 %collective-permute-start.2 = (bf16[192,1536]{1,0:T(8,128)(2,1)}, bf16[192,1536]{1,0:T(8,128)(2,1)}, u32[]{:S(2)}, u32[]{:S(2)}) collective-permute-start(bf16[192,1536]{1,0:T(8,128)(2,1)} %bitcast.13.fc00), channel_id=1, source_target_pairs={{0,4},{2,6},{4,0},{6,2},{8,12},{10,14},{12,8},{14,10},{16,20},{18,... | collective-permute-start | bytes 1769480 | tf_op jit(solution)/shard_map/ppermute | solution.py:218
  104.0 27.3 %collective-permute-start.3 = (bf16[192,1536]{1,0:T(8,128)(2,1)}, bf16[192,1536]{1,0:T(8,128)(2,1)}, u32[]{:S(2)}, u32[]{:S(2)}) collective-permute-start(bf16[192,1536]{1,0:T(8,128)(2,1)} %collective-permute-done.fc10), channel_id=1, source_target_pairs={{0,4},{2,6},{4,0},{6,2},{8,12},{10,14},{12,8},{14,10},{16,20},{18,... | collective-permute-start | bytes 1769480 | tf_op jit(solution)/shard_map/ppermute | solution.py:218
  104.5 23.3 %copy-start.14 = (s32[2048]{0:T(1024)}, s32[2048]{0:T(1024)S(1)}, u32[]{:S(2)}) copy-start(s32[2048]{0:T(1024)S(1)} %select_reduce_fusion) | copy-start | bytes 24580
  104.8 23.0 %copy-start.18 = (s32[17]{0:T(128)}, s32[17]{0:T(128)S(1)}, u32[]{:S(2)}) copy-start(s32[17]{0:T(128)S(1)} %pad_add_fusion.1.info) | copy-start | bytes 208
  129.3 73.8 %copy-start.12 = (bf16[1024,384]{1,0:T(8,128)(2,1)}, bf16[1024,384]{1,0:T(8,128)(2,1)S(1)}, u32[]{:S(2)}) copy-start(bf16[1024,384]{1,0:T(8,128)(2,1)S(1)} %get-tuple-element.121.orr) | copy-start | bytes 2359300
  131.2 12.1 %collective-permute-start.10 = (bf16[192,1536]{1,0:T(8,128)(2,1)}, bf16[192,1536]{1,0:T(8,128)(2,1)}, u32[]{:S(2)}, u32[]{:S(2)}) collective-permute-start(bf16[192,1536]{1,0:T(8,128)(2,1)} %collective-permute-done.2.fc01), channel_id=1, source_target_pairs={{0,2},{2,0},{4,6},{6,4},{8,10},{10,8},{12,14},{14,12},{16,18},{18,... | collective-permute-start | bytes 1769480 | tf_op jit(solution)/shard_map/ppermute | solution.py:218
  131.3 12.1 %collective-permute-start.11 = (bf16[192,1536]{1,0:T(8,128)(2,1)}, bf16[192,1536]{1,0:T(8,128)(2,1)}, u32[]{:S(2)}, u32[]{:S(2)}) collective-permute-start(bf16[192,1536]{1,0:T(8,128)(2,1)} %collective-permute-done.fc10), channel_id=1, source_target_pairs={{0,2},{2,0},{4,6},{6,4},{8,10},{10,8},{12,14},{14,12},{16,18},{18,... | collective-permute-start | bytes 1769480 | tf_op jit(solution)/shard_map/ppermute | solution.py:218
  131.8 15.5 %collective-permute-start.13 = (bf16[384,1536]{1,0:T(8,128)(2,1)}, bf16[384,1536]{1,0:T(8,128)(2,1)S(1)}, u32[]{:S(2)}, u32[]{:S(2)}) collective-permute-start(bf16[384,1536]{1,0:T(8,128)(2,1)} %pad_maximum_fusion.pr00), channel_id=1, source_target_pairs={{0,2},{2,0},{4,6},{6,4},{8,10},{10,8},{12,14},{14,12},{16,18},{18,... | collective-permute-start | bytes 3538952 | tf_op jit(solution)/shard_map/ppermute | solution.py:218
  131.8 15.5 %collective-permute-start.14 = (bf16[384,1536]{1,0:T(8,128)(2,1)}, bf16[384,1536]{1,0:T(8,128)(2,1)}, u32[]{:S(2)}, u32[]{:S(2)}) collective-permute-start(bf16[384,1536]{1,0:T(8,128)(2,1)} %collective-permute-done.4.pr10), channel_id=1, source_target_pairs={{0,2},{2,0},{4,6},{6,4},{8,10},{10,8},{12,14},{14,12},{16,18},{18,... | collective-permute-start | bytes 3538952 | tf_op jit(solution)/shard_map/ppermute | solution.py:218
  132.3 15.0 %collective-permute-start.7 = (bf16[1024,384]{1,0:T(8,128)(2,1)S(1)}, bf16[1024,384]{1,0:T(8,128)(2,1)S(1)}, u32[]{:S(2)}, u32[]{:S(2)}) collective-permute-start(bf16[1024,384]{1,0:T(8,128)(2,1)S(1)} %get-tuple-element.121.orr), channel_id=1, source_target_pairs={{0,2},{2,0},{4,6},{6,4},{8,10},{10,8},{12,14},{14,12},{16,18},{18,... | collective-permute-start | bytes 2359304 | tf_op jit(solution)/shard_map/ppermute | solution.py:218
  143.3 3.0 collective-permute-start.12
  143.3 3.9 %collective-permute-start.9 = (bf16[192,1536]{1,0:T(8,128)(2,1)}, bf16[192,1536]{1,0:T(8,128)(2,1)}, u32[]{:S(2)}, u32[]{:S(2)}) collective-permute-start(bf16[192,1536]{1,0:T(8,128)(2,1)} %bitcast.13.fc00), channel_id=1, source_target_pairs={{0,2},{2,0},{4,6},{6,4},{8,10},{10,8},{12,14},{14,12},{16,18},{18,... | collective-permute-start | bytes 1769480 | tf_op jit(solution)/shard_map/ppermute | solution.py:218
  203.0 4.8 %collective-permute-start.17 = (bf16[2,384,1536]{2,1,0:T(8,128)(2,1)}, bf16[2,384,1536]{2,1,0:T(8,128)(2,1)S(1)}, u32[]{:S(2)}, u32[]{:S(2)}) collective-permute-start(bf16[2,384,1536]{2,1,0:T(8,128)(2,1)} %get-tuple-element.115), channel_id=1, source_target_pairs={{0,2},{2,0},{4,6},{6,4},{8,10},{10,8},{12,14},{14,12},{16,18},{18,... | collective-permute-start | bytes 7077896 | tf_op jit(solution)/shard_map/ppermute | solution.py:218
  203.5 7.9 %collective-permute-start.16 = (bf16[2,384,1536]{2,1,0:T(8,128)(2,1)}, bf16[2,384,1536]{2,1,0:T(8,128)(2,1)S(1)}, u32[]{:S(2)}, u32[]{:S(2)}) collective-permute-start(bf16[2,384,1536]{2,1,0:T(8,128)(2,1)} %get-tuple-element.113), channel_id=1, source_target_pairs={{0,2},{2,0},{4,6},{6,4},{8,10},{10,8},{12,14},{14,12},{16,18},{18,... | collective-permute-start | bytes 7077896 | tf_op jit(solution)/shard_map/ppermute | solution.py:218
  203.6 9.4 %collective-permute-start.15 = (bf16[1024,384]{1,0:T(8,128)(2,1)}, bf16[1024,384]{1,0:T(8,128)(2,1)S(1)}, u32[]{:S(2)}, u32[]{:S(2)}) collective-permute-start(bf16[1024,384]{1,0:T(8,128)(2,1)} %get-tuple-element.111), channel_id=1, source_target_pairs={{0,2},{2,0},{4,6},{6,4},{8,10},{10,8},{12,14},{14,12},{16,18},{18,... | collective-permute-start | bytes 2359304 | tf_op jit(solution)/shard_map/ppermute | solution.py:218
  207.9 42.7 %copy-start.22 = (bf16[2,384,1536]{2,1,0:T(8,128)(2,1)}, bf16[2,384,1536]{2,1,0:T(8,128)(2,1)S(1)}, u32[]{:S(2)}) copy-start(bf16[2,384,1536]{2,1,0:T(8,128)(2,1)S(1)} %collective-permute-done.17) | copy-start | bytes 7077892
  211.4 41.9 %copy-start.23 = (bf16[2,384,1536]{2,1,0:T(8,128)(2,1)}, bf16[2,384,1536]{2,1,0:T(8,128)(2,1)S(1)}, u32[]{:S(2)}) copy-start(bf16[2,384,1536]{2,1,0:T(8,128)(2,1)S(1)} %collective-permute-done.16) | copy-start | bytes 7077892
  213.9 36.6 %collective-permute-start.19 = (bf16[384,1536]{1,0:T(8,128)(2,1)}, bf16[384,1536]{1,0:T(8,128)(2,1)S(1)}, u32[]{:S(2)}, u32[]{:S(2)}) collective-permute-start(bf16[384,1536]{1,0:T(8,128)(2,1)} %fusion), channel_id=1, source_target_pairs={{0,1},{1,0},{2,3},{3,2},{4,5},{5,4},{6,7},{7,6},{8,9},{9,8},{10,11... | collective-permute-start | bytes 3538952 | tf_op jit(solution)/shard_map/ppermute | solution.py:219
  215.6 34.9 %collective-permute-start.20 = (bf16[2,192,1536]{2,1,0:T(8,128)(2,1)}, bf16[2,192,1536]{2,1,0:T(8,128)(2,1)}, u32[]{:S(2)}, u32[]{:S(2)}) collective-permute-start(bf16[2,192,1536]{2,1,0:T(8,128)(2,1)} %add_convert_fusion), channel_id=1, source_target_pairs={{0,4},{2,6},{4,0},{6,2},{8,12},{10,14},{12,8},{14,10},{16,20},{18,... | collective-permute-start | bytes 3538952 | tf_op jit(solution)/shard_map/ppermute | solution.py:218
  250.5 23.6 %collective-permute-start.18 = (bf16[1024,1152]{1,0:T(8,128)(2,1)}, bf16[1024,1152]{1,0:T(8,128)(2,1)}, u32[]{:S(2)}, u32[]{:S(2)}) collective-permute-start(bf16[1024,1152]{1,0:T(8,128)(2,1)} %get-tuple-element.123), channel_id=1, source_target_pairs={{0,2},{2,0},{4,6},{6,4},{8,10},{10,8},{12,14},{14,12},{16,18},{18,... | collective-permute-start | bytes 7077896 | tf_op jit(solution)/shard_map/ppermute | solution.py:218
  254.3 16.2 %collective-permute-start.21 = (bf16[192,1536]{1,0:T(8,128)(2,1)}, bf16[192,1536]{1,0:T(8,128)(2,1)}, u32[]{:S(2)}, u32[]{:S(2)}) collective-permute-start(bf16[192,1536]{1,0:T(8,128)(2,1)} %fusion.4), channel_id=1, source_target_pairs={{0,4},{2,6},{4,0},{6,2},{8,12},{10,14},{12,8},{14,10},{16,20},{18,... | collective-permute-start | bytes 1769480 | tf_op jit(solution)/shard_map/ppermute | solution.py:218
  254.9 15.7 %collective-permute-start.22 = (bf16[192,1536]{1,0:T(8,128)(2,1)}, bf16[192,1536]{1,0:T(8,128)(2,1)S(1)}, u32[]{:S(2)}, u32[]{:S(2)}) collective-permute-start(bf16[192,1536]{1,0:T(8,128)(2,1)} %fusion.6), channel_id=1, source_target_pairs={{0,1},{1,0},{2,3},{3,2},{4,5},{5,4},{6,7},{7,6},{8,9},{9,8},{10,11... | collective-permute-start | bytes 1769480 | tf_op jit(solution)/shard_map/ppermute | solution.py:219
  255.2 96.6 %collective-permute-start.23 = (bf16[1024,768]{1,0:T(8,128)(2,1)}, bf16[1024,768]{1,0:T(8,128)(2,1)}, u32[]{:S(2)}, u32[]{:S(2)}) collective-permute-start(bf16[1024,768]{1,0:T(8,128)(2,1)} %get-tuple-element.109), channel_id=1, source_target_pairs={{1,2},{2,1},{5,6},{6,5},{9,10},{10,9},{13,14},{14,13},{17,18},{18,... | collective-permute-start | bytes 4718600 | tf_op jit(solution)/shard_map/ppermute | solution.py:1017
  274.1 16.6 %copy-start.8 = (bf16[384,1536]{1,0:T(8,128)(2,1)S(1)}, bf16[384,1536]{1,0:T(8,128)(2,1)}, u32[]{:S(2)}) copy-start(bf16[384,1536]{1,0:T(8,128)(2,1)} %get-tuple-element.144) | copy-start | bytes 3538948
  274.1 16.6 %copy-start.9 = (bf16[384,1536]{1,0:T(8,128)(2,1)S(1)}, bf16[384,1536]{1,0:T(8,128)(2,1)}, u32[]{:S(2)}) copy-start(bf16[384,1536]{1,0:T(8,128)(2,1)} %get-tuple-element.145) | copy-start | bytes 3538948
  (24 other events, 101.0 us)
